TPU v7x, 128 devices: a whole 4x4x4 slice. The times are simulated.
128 devices in a mesh: heads: 8 (over y, core), tokens: 8 (over x_hi, z), cols: 2 (over x_lo).
Axes of the slice: x: 4 (x_hi: 2, x_lo: 2; x = x_hi * 2 + x_lo), y: 4, z: 4, core: 2. Of those that a mesh axis runs over, the one named last changes fastest.
Arguments:
- query_in: bfloat16 [4096, 8192], P('tokens', ('heads', 'cols')), may hold values from -24 to 24
- key_in: bfloat16 [4096, 8192], P('tokens', ('heads', 'cols')), may hold values from -24 to 24
- value_in: bfloat16 [4096, 8192], P('tokens', ('heads', 'cols')), may hold values from -6 to 6
- out_grads: bfloat16 [4096, 8192], P('tokens', ('heads', 'cols')), may hold values from -6 to 6
- doc_starts: int32 [6], replicated, may hold values from 0 to 4095, as said below
Outputs:
- input_factor: float32 [8192, 8192], P('heads', ('tokens', 'cols'))
- grad_factor: float32 [8192, 8192], P('heads', ('tokens', 'cols'))
Inputs may be any that keep to these rules, and one draw needn't show every extreme that they name: Strictly increasing with the first entry 0; document d runs from doc_starts[d] to the next start (the last one to 4096) - 1. One document holds (8 // 2 + 1) * 512 tokens.
All inputs are finite; a program needn't handle non-finite values.
Results may differ from a plain program's by a relative error of at most 0.0041.
Values may be sent and summed in bfloat16 or wider, within the bound.
No kernel may reach another device: no remote copies, remote signals or barrier semaphores. Data moves between devices by JAX's collectives and lax.ppermute only.
A program may use at most 128 MiB of HBM per device.

v0:
```python
import math

import jax
import jax.numpy as jnp
from jax import lax
from jax.sharding import Mesh
from jax.sharding import PartitionSpec as P

HEAD_DIM = 128
TOKENS = ("tokens_0", "tokens_1")
TOKENS_COLS = ("tokens_0", "tokens_1", "cols")


MASK_FLOOR = -1e30


def side_by_side(arrays, axis, dim, along):
    widths = [a.shape[along] for a in arrays]
    both = jnp.concatenate(arrays, axis=along)
    result = lax.all_gather(both, axis, axis=dim, tiled=True)
    return tuple(jnp.split(result, [sum(widths[:k]) for k in range(1, len(widths))], axis=along))


def copy_for_each(shard, axis):
    count = lax.axis_size(axis)
    return lax.all_to_all(
        jnp.broadcast_to(shard[None], (count, *shard.shape)), axis, 0, 0, tiled=True
    )


def joined_along(tiles, dim):
    dims = list(tiles.shape[1:])
    dims[dim] *= tiles.shape[0]
    return jnp.moveaxis(tiles, 0, dim).reshape(dims)


def collect(shard, axis, dim):
    tiles = copy_for_each(shard, axis)
    return joined_along(tiles, dim)


def piece_ends(length, count):
    unit = 8 if length >= 8 * count else 1
    return [length // unit * k // count * unit for k in range(1, count)]


def all_blocks(shard, axes, sequence):
    tiles = shard[None]
    for k in sequence:
        tiles = lax.all_gather(tiles, axes[k], axis=0, tiled=True)
    block = [lax.axis_size(axes[k]) for k in reversed(sequence)]
    tiles = tiles.reshape(*block, *shard.shape)
    turned = sorted(range(len(sequence)), key=lambda place: sequence[len(sequence) - 1 - place])
    return tiles.transpose(*turned, *range(len(sequence), tiles.ndim)).reshape(-1, *shard.shape)


def gather_all_axes(shard, axes, dim):
    split_at = max(range(max(1, shard.ndim - 1)), key=lambda d: shard.shape[d])
    count, gathered = (len(axes), [])
    for initial, piece in enumerate(
        jnp.split(shard, piece_ends(shard.shape[split_at], count), axis=split_at)
    ):
        if piece.size:
            sequence = [(initial - k) % count for k in range(count)]
            gathered.append(all_blocks(piece, axes, sequence))
    return joined_along(jnp.concatenate(gathered, axis=split_at + 1), dim)


def padded_to(lines, count):
    spare = -lines.shape[0] % count
    if not spare:
        return lines
    return jnp.concatenate([lines, jnp.zeros((spare, *lines.shape[1:]), lines.dtype)])


def from_root(shard, axis, root):
    lines = jnp.where(lax.axis_index(axis) == root, shard, jnp.zeros_like(shard)).reshape(
        -1, *shard.shape[1:][-1:]
    )
    padded = padded_to(lines, lax.axis_size(axis))
    own = lax.psum_scatter(padded, axis, scatter_dimension=0, tiled=True)
    return lax.all_gather(own, axis, axis=0, tiled=True)[: len(lines)].reshape(shard.shape)


def document_ids(positions, doc_starts):
    return jnp.sum((positions[:, None] >= doc_starts[None, :]).astype(jnp.int32), axis=1) - 1


def doc_begin(position, doc_starts):
    return jnp.max(jnp.where(doc_starts <= position, doc_starts, 0))


def doc_finish(position, doc_starts, all_tokens):
    return jnp.min(jnp.where(doc_starts > position, doc_starts, all_tokens)) - 1


def pair_scores(query_rows, key_rows, query_pos, key_pos, doc_starts):
    head_count = query_rows.shape[1] // HEAD_DIM
    query_heads = query_rows.reshape(query_rows.shape[0], head_count, HEAD_DIM)
    key_heads = key_rows.reshape(key_rows.shape[0], head_count, HEAD_DIM)
    scores = jnp.einsum(
        "qhd,khd->hqk", query_heads, key_heads, preferred_element_type=jnp.float32
    ) * (1.0 / math.sqrt(HEAD_DIM))
    query_docs = document_ids(query_pos, doc_starts)
    key_docs = document_ids(key_pos, doc_starts)
    allowed = query_docs[:, None] == key_docs[None, :]
    return (scores, allowed[None, :, :])


def keep_state(running):
    return running


def on_device(query_in, key_in, value_in, out_grads, doc_starts):
    tok_dev, row_width = query_in.shape
    head_count = row_width // HEAD_DIM
    first_pos = lax.axis_index(TOKENS) * tok_dev
    query_pos = first_pos + jnp.arange(tok_dev, dtype=jnp.int32)
    highest = first_pos + tok_dev - 1
    lowest = doc_begin(first_pos, doc_starts)
    keys_all, values_all = side_by_side((key_in, value_in), TOKENS, 0, 1)
    all_tokens = keys_all.shape[0]
    furthest = doc_finish(highest, doc_starts, all_tokens)
    key_span = min(512, all_tokens)
    block_ids = jnp.arange(all_tokens // key_span, dtype=jnp.int32)

    def block_scores(block_id):
        key_begin = block_id * key_span
        key_rows = lax.dynamic_slice_in_dim(keys_all, key_begin, key_span, 0)
        key_pos = key_begin + jnp.arange(key_span, dtype=jnp.int32)
        scores, allowed = pair_scores(query_in, key_rows, query_pos, key_pos, doc_starts)
        return (key_begin, scores, allowed)

    def gated(block_id, update, running):
        key_begin = block_id * key_span
        reachable = (key_begin <= furthest) & (key_begin + key_span - 1 >= lowest)
        return lax.cond(reachable, update, keep_state, running)

    def stats_step(running, block_id):

        def update(state):
            row_peak, row_mass = state
            key_begin, scores, allowed = block_scores(block_id)
            masked = jnp.where(allowed, scores, MASK_FLOOR)
            new_peak = jnp.maximum(row_peak, jnp.max(masked, axis=2))
            new_mass = row_mass * jnp.exp(row_peak - new_peak) + jnp.sum(
                jnp.where(allowed, jnp.exp(masked - new_peak[:, :, None]), 0.0), axis=2
            )
            return (new_peak, new_mass)

        return (gated(block_id, update, running), None)

    initial = (
        jnp.full((head_count, tok_dev), MASK_FLOOR, jnp.float32),
        jnp.zeros((head_count, tok_dev), jnp.float32),
    )
    (row_peak, row_mass), _ = lax.scan(stats_step, initial, block_ids)
    log_total = row_peak + jnp.log(row_mass)

    def value_step(running, block_id):

        def update(state):
            weighted, partials = state
            key_begin, scores, allowed = block_scores(block_id)
            weights = jnp.where(allowed, jnp.exp(scores - log_total[:, :, None]), 0.0).astype(
                jnp.bfloat16
            )
            value_rows = lax.dynamic_slice_in_dim(values_all, key_begin, key_span, 0).reshape(
                key_span, head_count, HEAD_DIM
            )
            weighted = weighted + jnp.einsum(
                "hqk,khd->qhd", weights, value_rows, preferred_element_type=jnp.float32
            )
            return (weighted, partials)

        return (gated(block_id, update, running), None)

    partial_rows = 8
    value_init = (
        jnp.zeros((tok_dev, head_count, HEAD_DIM), jnp.float32),
        jnp.zeros((partial_rows, row_width), jnp.float32),
    )
    (weighted, partials), _ = lax.scan(value_step, value_init, block_ids)
    attended = weighted.reshape(tok_dev, row_width).astype(jnp.bfloat16)
    stats_all = collect(log_total.T, TOKENS, 0)
    piece_start = jnp.int32(0)
    query_rows, grad_rows = side_by_side((query_in, out_grads), TOKENS, 0, 1)
    piece_rows = query_rows.shape[0]
    piece_pos = jnp.arange(piece_rows, dtype=jnp.int32)

    def update(grad_sum):
        scores, allowed = pair_scores(query_rows, key_in, piece_pos, query_pos, doc_starts)
        weights = jnp.where(allowed, jnp.exp(scores - stats_all.T[:, :, None]), 0.0).astype(
            jnp.bfloat16
        )
        piece_grads = grad_rows.reshape(piece_rows, head_count, HEAD_DIM)
        return jnp.einsum("hqk,qhd->khd", weights, piece_grads, preferred_element_type=jnp.float32)

    reachable = (piece_start + piece_rows - 1 >= lowest) & (piece_start <= furthest)
    summed = lax.cond(
        reachable, update, keep_state, jnp.zeros((tok_dev, head_count, HEAD_DIM), jnp.float32)
    )
    value_grads = summed.reshape(tok_dev, row_width).astype(jnp.bfloat16)
    token_shards = lax.axis_size(TOKENS)
    col_shards = lax.axis_size("cols")
    rows_attended, rows_grads = (
        gather_all_axes(attended[None], TOKENS_COLS, 0),
        gather_all_axes(value_grads[None], TOKENS_COLS, 0),
    )
    rows_attended = rows_attended.reshape(token_shards, col_shards, tok_dev, row_width)
    rows_grads = rows_grads.reshape(token_shards, col_shards, tok_dev, row_width)
    own_attended = lax.dynamic_index_in_dim(
        rows_attended, lax.axis_index("cols"), 1, keepdims=False
    )
    own_grads = lax.dynamic_index_in_dim(rows_grads, lax.axis_index("cols"), 1, keepdims=False)
    cols_attended, cols_grads = (
        from_root(own_attended, "heads", lax.axis_index(TOKENS)),
        from_root(own_grads, "heads", lax.axis_index(TOKENS)),
    )
    input_factor = jnp.einsum(
        "acnf,ang->cfg", rows_attended, cols_attended, preferred_element_type=jnp.float32
    )
    grad_factor = jnp.einsum(
        "acnf,ang->cfg", rows_grads, cols_grads, preferred_element_type=jnp.float32
    )
    input_factor = input_factor.reshape(col_shards * row_width, row_width) / all_tokens
    grad_factor = grad_factor.reshape(col_shards * row_width, row_width) / all_tokens
    return (input_factor, grad_factor)


def solution(mesh):
    split = Mesh(
        mesh.devices.reshape(mesh.shape["heads"], 2, 4, mesh.shape["cols"]),
        ("heads", "tokens_0", "tokens_1", "cols"),
    )
    in_specs = (
        P(TOKENS, ("heads", "cols")),
        P(TOKENS, ("heads", "cols")),
        P(TOKENS, ("heads", "cols")),
        P(TOKENS, ("heads", "cols")),
        P(),
    )
    out_specs = (P("heads", TOKENS_COLS), P("heads", TOKENS_COLS))
    return jax.shard_map(
        on_device, mesh=split, in_specs=in_specs, out_specs=out_specs, check_vma=False
    )
```

profile of v0, /device:TPU:24, one launch (start us, length us, event | category | flops | bytes accessed | tf_op | source)
XLA Modules:
  0.0 782.6 jit_solution(14680790935058764619)
XLA Ops:
  14.0 112.7 %all-gather.33.cloned.1.call-done = bf16[4096,1024]{0,1:T(8,128)(2,1)} async-done(((bf16[512,1024]{0,1:T(8,128)(2,1)}), bf16[4096,1024]{0,1:T(8,128)(2,1)}) %all-gather.33.cloned.1.call-update) | async-done | bytes 8388624 | tf_op jit(solution)/shard_map/all_gather | solution.py:20
  132.6 23.9 %while.35 = (s32[]{:T(128)}, f32[4,512]{1,0:T(4,128)S(1)}, f32[4,512]{1,0:T(4,128)S(1)}, s32[8]{0:T(128)S(1)}, s32[]{:T(128)}, /*index=5*/s32[]{:T(128)}, s32[6]...) while((s32[]{:T(128)}, f32[4,512]{1,0:T(4,128)S(1)}, ...), condition=%wide.region_9.10_spmd.clone, body=%wide.region_2.9_spmd.clone.sunk | while | flops 277109760 | bytes 11407741 | solution.py:157
  156.7 23.2 %while.36 = (s32[]{:T(128)}, f32[512,4,128]{0,2,1:T(8,128)S(1)}, s32[8]{0:T(128)S(1)}, s32[]{:T(128)}, s32[]{:T(128)}, /*index=5*/bf16[4096,512]{0,1:T(8,128)(2,...) while((s32[]{:T(128)}, f32[512,4,128]{0,2,1:T(8,128)S(1)}, ...), condition=%wide.region_15.16_spmd.clone, body=%wide.region_10.15_spmd.clone.sunk | while | flops 541608960 | bytes 6328685 | solution.py:183
  180.2 56.0 %all-gather.3 = bf16[4,168,512]{2,1,0:T(8,128)(2,1)} all-gather(bf16[1,168,512]{2,1,0:T(8,128)(2,1)S(1)} %copy.127), channel_id=5, replica_groups=mesh['heads'=8,'tokens_0'=2,'tokens_1'=4,'cols'=2] {'tokens_1'}, dimensions={0}, use_global_device_ids=true | all-gather | bytes 860160 | tf_op jit(solution)/shard_map/all_gather | solution.py:50
  254.7 26.2 %conditional.3 = (bf16[512,4,128]{2,0,1:T(8,128)(2,1)S(1)}) conditional(s32[]{:T(128)} %convert_element_type.73, () %tuple.75, (s32[4096]{0:T(1024)S(1)}, s32[6]{0:T(128)S(1)}, s32[]{:T(128)}, bf16[4096,1024]{0,1:T(8,128)(2,1)}, bf16[512,512]{1,0:T(8,128)(2,1)S(1)}, /*index=5*/f32[8,512,4]{1,2,0:T(4,128)S(1)}, s32[512]{0:T(512)S(1)}) %tuple.181), branch_computations={%region_17.18_spmd, %region_18.0_spmd} | conditional | flops 4330702336 | bytes 30570556 | solution.py:200
  263.0 17.8 %fusion.22 = bf16[512,4,128]{2,0,1:T(8,128)(2,1)S(1)} fusion(bf16[4096,4,128]{0,2,1:T(8,128)(2,1)} %bitcast.119, f32[4,4096]{1,0:T(4,128)S(1)} %bitcast.130, pred[4096,512]{1,0:T(8,128)(4,1)S(1)} %broadcast_compare_fusion.2, bf16[4096,4,128]{0,2,1:T(8,128)(2,1)} %bitcast.118, bf16[512,512]{1,0:T(8,128)(2,1)S(1)} %get-tuple-element.507), kind=kOutput, calls=%fused_computation.40 | convolution fusion | flops 4328521728 | bytes 11599872 | tf_op jit(solution)/shard_map/cond/branch_1_fun/hqk,qhd->khd/dot_general | solution.py:197
  281.4 16.7 %all-gather.12 = bf16[4,168,512]{2,1,0:T(8,128)(2,1)} all-gather(bf16[1,168,512]{2,1,0:T(8,128)(2,1)S(1)} %copy.115), channel_id=14, replica_groups=mesh['heads'=8,'tokens_0'=2,'tokens_1'=4,'cols'=2] {'tokens_1'}, dimensions={0}, use_global_device_ids=true | all-gather | bytes 860160 | tf_op jit(solution)/shard_map/all_gather | solution.py:50
  313.3 15.4 %all-gather.1 = bf16[4,168,512]{2,1,0:T(8,128)(2,1)} all-gather(bf16[2,168,512]{2,1,0:T(8,128)(2,1)S(1)} %all-gather), channel_id=3, replica_groups=mesh['heads'=8,'tokens_0'=2,'tokens_1'=4,'cols'=2] {'cols'}, dimensions={0}, use_global_device_ids=true | all-gather | bytes 1032192 | tf_op jit(solution)/shard_map/all_gather | solution.py:50
  341.9 9.7 %all-gather.10 = bf16[4,168,512]{2,1,0:T(8,128)(2,1)} all-gather(bf16[2,168,512]{2,1,0:T(8,128)(2,1)S(1)} %all-gather.9), channel_id=12, replica_groups=mesh['heads'=8,'tokens_0'=2,'tokens_1'=4,'cols'=2] {'cols'}, dimensions={0}, use_global_device_ids=true | all-gather | bytes 1032192 | tf_op jit(solution)/shard_map/all_gather | solution.py:50
  351.6 8.4 %all-gather.57.cloned.1.call-done = bf16[8,176,512]{2,1,0:T(8,128)(2,1)} async-done(((bf16[2,176,512]{2,1,0:T(8,128)(2,1)}), bf16[8,176,512]{2,1,0:T(8,128)(2,1)}) %all-gather.57.cloned.1.call-update) | async-done | bytes 1441808 | tf_op jit(solution)/shard_map/all_gather | solution.py:50
  360.1 45.0 %all-gather.45.cloned.1.call-done = bf16[16,168,512]{2,1,0:T(8,128)(2,1)} async-done(((bf16[8,168,512]{2,1,0:T(8,128)(2,1)}), bf16[16,168,512]{2,1,0:T(8,128)(2,1)}) %all-gather.45.cloned.1.call-update) | async-done | bytes 2752528 | tf_op jit(solution)/shard_map/all_gather | solution.py:50
  407.2 37.1 %all-gather.41.cloned.1.call-done = bf16[16,168,512]{2,1,0:T(8,128)(2,1)} async-done(((bf16[4,168,512]{2,1,0:T(8,128)(2,1)}), bf16[16,168,512]{2,1,0:T(8,128)(2,1)}) %all-gather.41.cloned.1.call-update) | async-done | bytes 2752528 | tf_op jit(solution)/shard_map/all_gather | solution.py:50
  448.0 44.0 %all-gather.49.cloned.1.call-done = bf16[16,176,512]{2,1,0:T(8,128)(2,1)} async-done(((bf16[8,176,512]{2,1,0:T(8,128)(2,1)}), bf16[16,176,512]{2,1,0:T(8,128)(2,1)}) %all-gather.49.cloned.1.call-update) | async-done | bytes 2883600 | tf_op jit(solution)/shard_map/all_gather | solution.py:50
  501.2 34.7 %all-gather.55.cloned.1.call-done = bf16[16,168,512]{2,1,0:T(8,128)(2,1)} async-done(((bf16[8,168,512]{2,1,0:T(8,128)(2,1)}), bf16[16,168,512]{2,1,0:T(8,128)(2,1)}) %all-gather.55.cloned.1.call-update) | async-done | bytes 2752528 | tf_op jit(solution)/shard_map/all_gather | solution.py:50
  538.0 37.1 %all-gather.51.cloned.1.call-done = bf16[16,168,512]{2,1,0:T(8,128)(2,1)} async-done(((bf16[4,168,512]{2,1,0:T(8,128)(2,1)}), bf16[16,168,512]{2,1,0:T(8,128)(2,1)}) %all-gather.51.cloned.1.call-update) | async-done | bytes 2752528 | tf_op jit(solution)/shard_map/all_gather | solution.py:50
  578.8 43.8 %all-gather.59.cloned.1.call-done = bf16[16,176,512]{2,1,0:T(8,128)(2,1)} async-done(((bf16[8,176,512]{2,1,0:T(8,128)(2,1)}), bf16[16,176,512]{2,1,0:T(8,128)(2,1)}) %all-gather.59.cloned.1.call-update) | async-done | bytes 2883600 | tf_op jit(solution)/shard_map/all_gather | solution.py:50
  631.6 27.1 %reduce-scatter.3.cloned.1.call-done = bf16[512,512]{1,0:T(8,128)(2,1)} async-done(((bf16[4096,512]{1,0:T(8,128)(2,1)}), bf16[512,512]{1,0:T(8,128)(2,1)}) %reduce-scatter.3.cloned.1.call-update) | async-done | bytes 524304 | tf_op jit(solution)/shard_map/reduce_scatter | solution.py:81
  658.8 38.9 %reduce-scatter.5.cloned.1.call-done = bf16[512,512]{1,0:T(8,128)(2,1)} async-done(((bf16[4096,512]{1,0:T(8,128)(2,1)}), bf16[512,512]{1,0:T(8,128)(2,1)}) %reduce-scatter.5.cloned.1.call-update) | async-done | bytes 524304 | tf_op jit(solution)/shard_map/reduce_scatter | solution.py:81
  697.8 12.3 %copy.108 = bf16[2,512,8,512]{3,1,0,2:T(8,128)(2,1)} copy(bf16[2,512,8,512]{1,3,0,2:T(8,128)(2,1)} %get-tuple-element.702) | data formatting | bytes 16777216 | tf_op jit(solution)/shard_map/acnf,ang->cfg/dot_general | solution.py:220
  710.1 12.5 %copy.118 = bf16[2,512,8,512]{3,1,0,2:T(8,128)(2,1)} copy(bf16[2,512,8,512]{1,3,0,2:T(8,128)(2,1)} %get-tuple-element.700) | data formatting | bytes 16777216 | tf_op jit(solution)/shard_map/acnf,ang->cfg/dot_general | solution.py:223
  722.6 9.5 %all-gather.35.cloned.1.call-done = bf16[4096,512]{1,0:T(8,128)(2,1)} async-done(((bf16[512,512]{1,0:T(8,128)(2,1)}), bf16[4096,512]{1,0:T(8,128)(2,1)}) %all-gather.35.cloned.1.call-update) | async-done | bytes 4194320 | tf_op jit(solution)/shard_map/all_gather | solution.py:82
  732.1 10.4 %bitcast_multiply_fusion.1 = f32[1024,512]{1,0:T(8,128)} fusion(bf16[1024,8,512]{2,0,1:T(8,128)(2,1)} %bitcast.117, bf16[8,512,512]{2,1,0:T(8,128)(2,1)} %bitcast.132), kind=kOutput, calls=%fused_computation.55 | convolution fusion | flops 4295491584 | bytes 14680064 | tf_op jit(solution)/shard_map/acnf,ang->cfg/dot_general | solution.py:220
  742.4 23.3 %all-gather.39.cloned.1.call-done = bf16[4096,512]{1,0:T(8,128)(2,1)} async-done(((bf16[512,512]{1,0:T(8,128)(2,1)}), bf16[4096,512]{1,0:T(8,128)(2,1)}) %all-gather.39.cloned.1.call-update) | async-done | bytes 4194320 | tf_op jit(solution)/shard_map/all_gather | solution.py:82
  765.7 10.4 %bitcast_multiply_fusion = f32[1024,512]{1,0:T(8,128)} fusion(bf16[1024,8,512]{2,0,1:T(8,128)(2,1)} %bitcast.116, bf16[8,512,512]{2,1,0:T(8,128)(2,1)} %bitcast.133), kind=kOutput, calls=%fused_computation.54 | convolution fusion | flops 4295491584 | bytes 14680064 | tf_op jit(solution)/shard_map/acnf,ang->cfg/dot_general | solution.py:223
  (178 shorter events, 136.2 us)
Async XLA Ops:
  7.2 3.8 copy-start.1
  7.2 4.0 copy-start
  7.2 119.4 %all-gather.33.cloned.1.call-start = ((), (), s32[]{:S(2)}) async-start(), calls=%async_computation.3 | async-start | bytes 9437184 | tf_op jit(solution)/shard_map/all_gather | solution.py:20
  9.8 2.7 copy-start.3
  10.9 236.7 %all-gather.37.cloned.1.call-start = ((), (), s32[]{:S(2)}) async-start(), calls=%async_computation.6 | async-start | bytes 9437184 | tf_op jit(solution)/shard_map/all_gather | solution.py:20
  12.5 292.4 %all-gather.43.cloned.1.call-start = ((), (), s32[]{:S(2)}) async-start(), calls=%async_computation.10 | async-start | bytes 2064384 | tf_op jit(solution)/shard_map/all_gather | solution.py:50
  179.9 74.8 %copy-start.2 = (bf16[512,512]{1,0:T(8,128)(2,1)S(1)}, bf16[512,512]{1,0:T(8,128)(2,1)}, u32[]{:S(2)}) copy-start(bf16[512,512]{1,0:T(8,128)(2,1)} %param.16) | copy-start | bytes 1572868
  236.3 92.4 %all-gather.47.cloned.1.call-start = ((), (), s32[]{:S(2)}) async-start(), calls=%async_computation.12 | async-start | bytes 1802240 | tf_op jit(solution)/shard_map/all_gather | solution.py:50
  243.5 11.1 %all-to-all-start = ((f32[8,512,4]{1,2,0:T(4,128)}), f32[8,512,4]{1,2,0:T(4,128)S(1)}, u32[]{:S(2)}, u32[]{:S(2)}) async-start(f32[8,512,4]{1,2,0:T(4,128)} %broadcast_in_dim.108), calls=%async_computation.1 | async-start | bytes 131072 | tf_op jit(solution)/shard_map/all_to_all | solution.py:26
  246.9 86.5 %all-gather.53.cloned.1.call-start = ((), (), s32[]{:S(2)}) async-start(), calls=%async_computation.15 | async-start | bytes 2064384 | tf_op jit(solution)/shard_map/all_gather | solution.py:50
  298.1 61.9 %all-gather.57.cloned.1.call-start = ((), (), s32[]{:S(2)}) async-start(), calls=%async_computation.17 | async-start | bytes 1802240 | tf_op jit(solution)/shard_map/all_gather | solution.py:50
  304.8 100.4 %all-gather.45.cloned.1.call-start = ((), (), s32[]{:S(2)}) async-start(), calls=%async_computation.11 | async-start | bytes 4128768 | tf_op jit(solution)/shard_map/all_gather | solution.py:50
  305.5 138.8 %all-gather.41.cloned.1.call-start = ((), (), s32[]{:S(2)}) async-start(), calls=%async_computation.9 | async-start | bytes 3440640 | tf_op jit(solution)/shard_map/all_gather | solution.py:50
  328.7 163.3 %all-gather.49.cloned.1.call-start = ((), (), s32[]{:S(2)}) async-start(), calls=%async_computation.13 | async-start | bytes 4325376 | tf_op jit(solution)/shard_map/all_gather | solution.py:50
  329.4 206.6 %all-gather.55.cloned.1.call-start = ((), (), s32[]{:S(2)}) async-start(), calls=%async_computation.16 | async-start | bytes 4128768 | tf_op jit(solution)/shard_map/all_gather | solution.py:50
  333.4 241.7 %all-gather.51.cloned.1.call-start = ((), (), s32[]{:S(2)}) async-start(), calls=%async_computation.14 | async-start | bytes 3440640 | tf_op jit(solution)/shard_map/all_gather | solution.py:50
  351.6 271.1 %all-gather.59.cloned.1.call-start = ((), (), s32[]{:S(2)}) async-start(), calls=%async_computation.18 | async-start | bytes 4325376 | tf_op jit(solution)/shard_map/all_gather | solution.py:50
  360.1 298.7 %reduce-scatter.3.cloned.1.call-start = ((), (), s32[]{:S(2)}) async-start(), calls=%async_computation.4 | async-start | bytes 4718592 | tf_op jit(solution)/shard_map/reduce_scatter | solution.py:81
  500.9 196.8 %reduce-scatter.5.cloned.1.call-start = ((), (), s32[]{:S(2)}) async-start(), calls=%async_computation.7 | async-start | bytes 4718592 | tf_op jit(solution)/shard_map/reduce_scatter | solution.py:81
  631.6 100.5 %all-gather.35.cloned.1.call-start = ((), (), s32[]{:S(2)}) async-start(), calls=%async_computation.5 | async-start | bytes 4718592 | tf_op jit(solution)/shard_map/all_gather | solution.py:82
  658.8 107.0 %all-gather.39.cloned.1.call-start = ((), (), s32[]{:S(2)}) async-start(), calls=%async_computation.8 | async-start | bytes 4718592 | tf_op jit(solution)/shard_map/all_gather | solution.py:82
Sparse Core Ops, SparseCore 0:
  11.0 115.5 all-gather.32
  129.4 113.0 all-gather.36
  244.2 26.2 all-gather.42
  271.9 28.7 all-gather.46
  302.3 31.0 all-gather.52
  334.9 25.1 all-gather.56
  361.7 43.3 all-gather.44
  406.8 37.4 all-gather.40
  446.0 45.9 all-gather.48
  493.5 42.4 all-gather.54
  537.6 37.4 all-gather.50
  576.6 45.9 all-gather.58
  625.0 33.6 reduce-scatter.2
  661.0 36.6 reduce-scatter.4
  699.3 32.7 all-gather.34
  733.6 32.0 all-gather.38
where the time goes:
time: 788 us; the launch traced here: 783 us
  waiting for transfers between devices  474 us (60%)
  blocking collectives  126 us (16%)
  local copies, waits for them, and re-layouts  67.7 us (9%)
  matrix products  43.8 us (6%)
  other arithmetic  26.3 us (3%)
  loops' own time  24.5 us (3%)
  between operations  15.6 us (2%)
    all_gather x10, waiting for transfers between devices, all_blocks(): tiles = lax.all_gather(tiles, axes[k], axis=0, tiled=True)  254 us
    all_gather x8, blocking collectives, all_blocks(): tiles = lax.all_gather(tiles, axes[k], axis=0, tiled=True)  126 us
    all_gather x2, waiting for transfers between devices, side_by_side(): result = lax.all_gather(both, axis, axis=dim, tiled=True)  113 us
    reduce_scatter x2, waiting for transfers between devices, from_root(): own = lax.psum_scatter(padded, axis, scatter_dimension=0, tiled=True)  66 us
    all_gather x2, waiting for transfers between devices, from_root(): lax.all_gather(own, axis, axis=0, tiled=True)[:len(lines)]  32.8 us
    dot_general x1, matrix products, update(): jnp.einsum('hqk,qhd->khd', weights, piece_grads, preferred_element_type=j...  17.8 us
  transfers between devices with their start and end apart: 17, of which 14 were waited for; matrix products, arithmetic and copies ran while one was open for 16% of the time, Pallas kernels for 0%

commit v1 on v0

v1 whole, which is shorter than its diff:
```python
import math

import jax
import jax.numpy as jnp
from jax import lax
from jax.experimental import pallas as pl
from jax.experimental.pallas import tpu as pltpu
from jax.sharding import Mesh
from jax.sharding import PartitionSpec as P

HEAD_DIM = 128
X = ("xh", "xl")
MASK_FLOOR = -1e30
KEY_STEP = 512
QUERY_STEP = 256
VMEM_BYTES = 56 * 1024 * 1024


def attention_kernel(
    starts, where_ref, q_ref, g_ref, k_own, k_oth, v_own, v_oth,
    att_ref, near_ref, far_ref,
    k_all, v_all, v_turned, scores, grads, sems,
):
    half = q_ref.shape[0]
    half_id = where_ref[0]
    own_at = pl.multiple_of(half_id * half, half)
    oth_at = pl.multiple_of((1 - half_id) * half, half)
    copies = [
        pltpu.make_async_copy(k_own, k_all.at[pl.ds(own_at, half)], sems.at[0]),
        pltpu.make_async_copy(k_oth, k_all.at[pl.ds(oth_at, half)], sems.at[1]),
        pltpu.make_async_copy(v_own, v_all.at[pl.ds(own_at, half)], sems.at[2]),
        pltpu.make_async_copy(v_oth, v_all.at[pl.ds(oth_at, half)], sems.at[3]),
    ]
    for copy in copies:
        copy.start()
    grads[...] = jnp.zeros_like(grads)
    for copy in copies:
        copy.wait()
    all_tokens = 2 * half
    docs = starts.shape[0]
    for at in range(0, all_tokens, KEY_STEP):
        v_turned[:, at : at + KEY_STEP] = v_all[at : at + KEY_STEP, :].T
    scale = math.log2(math.e) / math.sqrt(HEAD_DIM)
    groups = KEY_STEP // 8

    def query_block(block, carry):
        row = pl.multiple_of(block * QUERY_STEP, QUERY_STEP)
        first = own_at + row
        last = first + QUERY_STEP - 1
        pos = first + lax.broadcasted_iota(jnp.int32, (1, QUERY_STEP), 1)
        begin = jnp.zeros((1, QUERY_STEP), jnp.int32)
        finish = jnp.full((1, QUERY_STEP), all_tokens, jnp.int32)
        lowest = jnp.int32(0)
        highest = jnp.int32(all_tokens)
        for d in range(docs):
            start = starts[d]
            lowest = jnp.where(start <= first, jnp.maximum(lowest, start), lowest)
            highest = jnp.where(start > last, jnp.minimum(highest, start), highest)
            begin = jnp.where(start <= pos, jnp.maximum(begin, start), begin)
            finish = jnp.where(start > pos, jnp.minimum(finish, start), finish)
        step_from = lowest // KEY_STEP
        step_to = (highest + KEY_STEP - 1) // KEY_STEP
        queries = q_ref[pl.ds(row, QUERY_STEP), :]
        cotangents = g_ref[pl.ds(row, QUERY_STEP), :]
        key_iota = lax.broadcasted_iota(jnp.int32, (KEY_STEP, QUERY_STEP), 0)

        def score_step(step, peak):
            at = pl.multiple_of(step * KEY_STEP, KEY_STEP)
            s = lax.dot_general(
                k_all[pl.ds(at, KEY_STEP), :], queries, (((1,), (1,)), ((), ())),
                preferred_element_type=jnp.float32,
            ) * scale
            allowed = (key_iota >= begin - at) & (key_iota < finish - at)
            s = jnp.where(allowed, s, MASK_FLOOR)
            scores[pl.ds(at, KEY_STEP), :] = s
            return jnp.maximum(peak, jnp.max(s.reshape(groups, 8, QUERY_STEP), axis=0))

        peak = lax.fori_loop(
            step_from, step_to, score_step, jnp.full((8, QUERY_STEP), MASK_FLOOR, jnp.float32)
        )
        peak = jnp.max(peak, axis=0, keepdims=True)

        def mass_step(step, mass):
            at = pl.multiple_of(step * KEY_STEP, KEY_STEP)
            e = jnp.exp2(scores[pl.ds(at, KEY_STEP), :] - peak)
            scores[pl.ds(at, KEY_STEP), :] = e
            return mass + jnp.sum(e.reshape(groups, 8, QUERY_STEP), axis=0)

        mass = lax.fori_loop(step_from, step_to, mass_step, jnp.zeros((8, QUERY_STEP), jnp.float32))
        share = 1.0 / jnp.sum(mass, axis=0, keepdims=True)

        def value_step(step, summed):
            at = pl.multiple_of(step * KEY_STEP, KEY_STEP)
            w = (scores[pl.ds(at, KEY_STEP), :] * share).astype(jnp.bfloat16)
            grads[pl.ds(at, KEY_STEP), :] += jnp.dot(
                w, cotangents, preferred_element_type=jnp.float32
            )
            return summed + jnp.dot(
                v_turned[:, pl.ds(at, KEY_STEP)], w, preferred_element_type=jnp.float32
            )

        summed = lax.fori_loop(
            step_from, step_to, value_step, jnp.zeros((HEAD_DIM, QUERY_STEP), jnp.float32)
        )
        att_ref[:, pl.ds(row, QUERY_STEP)] = summed.astype(jnp.bfloat16)
        return carry

    lax.fori_loop(0, half // QUERY_STEP, query_block, 0)
    for at in range(0, half, KEY_STEP):
        near_ref[:, at : at + KEY_STEP] = grads[pl.ds(own_at + at, KEY_STEP), :].T
        far_ref[:, at : at + KEY_STEP] = grads[pl.ds(oth_at + at, KEY_STEP), :].T


def attention(starts, half_id, q, g, k_own, k_oth, v_own, v_oth):
    half = q.shape[0]
    hbm = pl.BlockSpec(memory_space=pl.ANY)
    vmem = pl.BlockSpec(memory_space=pltpu.VMEM)
    smem = pl.BlockSpec(memory_space=pltpu.SMEM)
    return pl.pallas_call(
        attention_kernel,
        out_shape=(
            jax.ShapeDtypeStruct((HEAD_DIM, half), jnp.bfloat16),
            jax.ShapeDtypeStruct((HEAD_DIM, half), jnp.float32),
            jax.ShapeDtypeStruct((HEAD_DIM, half), jnp.float32),
        ),
        in_specs=[smem, smem, vmem, vmem, hbm, hbm, hbm, hbm],
        out_specs=(vmem, vmem, vmem),
        scratch_shapes=[
            pltpu.VMEM((2 * half, HEAD_DIM), jnp.bfloat16),
            pltpu.VMEM((2 * half, HEAD_DIM), jnp.bfloat16),
            pltpu.VMEM((HEAD_DIM, 2 * half), jnp.bfloat16),
            pltpu.VMEM((2 * half, QUERY_STEP), jnp.float32),
            pltpu.VMEM((2 * half, HEAD_DIM), jnp.float32),
            pltpu.SemaphoreType.DMA((4,)),
        ],
        compiler_params=pltpu.CompilerParams(vmem_limit_bytes=VMEM_BYTES),
        name="attention",
    )(starts, half_id, q, g, k_own, k_oth, v_own, v_oth)


def shifted(x, axis, by):
    count = lax.axis_size(axis)
    return lax.ppermute(x, axis, [(i, (i + by) % count) for i in range(count)])


def ring(x, axis):
    half = x.shape[0] // 2
    below, above = shifted(x, axis, 1), shifted(x, axis, -1)
    far = (shifted(below[:half], axis, 1), shifted(above[half:], axis, -1))
    return (x, below, above, *far)


def stack_kernel(*refs):
    count = len(refs) - 2
    parts, out, sems = refs[:count], refs[count], refs[count + 1]
    copies, at = [], 0
    for k, part in enumerate(parts):
        rows = part.shape[0]
        copies.append(pltpu.make_async_copy(part, out.at[pl.ds(at, rows)], sems.at[k]))
        at += rows
    for copy in copies:
        copy.start()
    for copy in copies:
        copy.wait()


def stacked(parts):
    rows = sum(p.shape[0] for p in parts)
    hbm = pl.BlockSpec(memory_space=pl.ANY)
    return pl.pallas_call(
        stack_kernel,
        out_shape=jax.ShapeDtypeStruct((rows, *parts[0].shape[1:]), parts[0].dtype),
        in_specs=[hbm] * len(parts),
        out_specs=hbm,
        scratch_shapes=[pltpu.SemaphoreType.DMA((len(parts),))],
        name="stack",
    )(*parts)


def factor_kernel(place, *refs, z_first, count):
    row_refs, own_cols, oth_cols = refs[:5], refs[5:10], refs[10:15]
    out, rows, cols, sems = refs[15], refs[16], refs[17], refs[18]
    x, y, z, core = place[0], place[1], place[2], place[3]
    block = HEAD_DIM
    half = block // 2
    copies = []

    def start(src, dst):
        copy = pltpu.make_async_copy(src, dst, sems.at[len(copies)])
        copy.start()
        copies.append(copy)

    ring_steps = (0, 3, 1, 2)
    for who, parts in ((core, own_cols), (1 - core, oth_cols)):
        for k in range(5):
            if k < 3:
                at = pl.multiple_of(((y + ring_steps[k]) % 4) * block, block)
                start(parts[k], cols.at[who, pl.ds(at, block)])
            else:
                at = pl.multiple_of(((y + 2) % 4) * block + (k - 3) * half, half)
                start(parts[k], cols.at[who, pl.ds(at, half)])
    for k in range(5):
        outer = ring_steps[min(k, 3)]
        inners = ((0, 1, 2, 3), (0, 1, 2, 3), (0, 1, 2, 3), (0, 1), (2, 3))[k]
        for n, slot in enumerate(inners):
            inner = ring_steps[slot]
            zz = (z + (inner if z_first else outer)) % 4
            xx = (x + (outer if z_first else inner)) % 4
            at = pl.multiple_of(((xx % 2) * 4 + zz) * block, block)
            start(row_refs[k].at[pl.ds(n * block, block)], rows.at[xx // 2, pl.ds(at, block)])
    for copy in copies:
        copy.wait()
    step = 256
    for at in range(0, rows.shape[1], step):
        total = None
        for who in range(2):
            part = lax.dot_general(
                rows[who, at : at + step, :], cols[who], (((1,), (1,)), ((), ())),
                preferred_element_type=jnp.float32,
            )
            total = part if total is None else total + part
        out[at : at + step, :] = total * (1.0 / count)


def factor(place, rows, own_cols, oth_cols, z_first, count):
    tokens = own_cols[0].shape[1]
    hbm = pl.BlockSpec(memory_space=pl.ANY)
    kernel = lambda *refs: factor_kernel(*refs, z_first=z_first, count=count)
    return pl.pallas_call(
        kernel,
        out_shape=jax.ShapeDtypeStruct((8 * HEAD_DIM, 4 * HEAD_DIM), jnp.float32),
        in_specs=[pl.BlockSpec(memory_space=pltpu.SMEM)] + [hbm] * 15,
        out_specs=pl.BlockSpec(memory_space=pltpu.VMEM),
        scratch_shapes=[
            pltpu.VMEM((2, 8 * HEAD_DIM, tokens), jnp.bfloat16),
            pltpu.VMEM((2, 4 * HEAD_DIM, tokens), jnp.bfloat16),
            pltpu.SemaphoreType.DMA((26,)),
        ],
        compiler_params=pltpu.CompilerParams(vmem_limit_bytes=VMEM_BYTES),
        name="factor_z_first" if z_first else "factor_x_first",
    )(place, *rows, *own_cols, *oth_cols)


def by_head(x):
    return lax.all_to_all(x, "z", split_axis=1, concat_axis=0, tiled=True)


def column_moves():
    def index(y, core, xh, z):
        return ((y * 2 + core) * 2 + xh) * 4 + z

    moves = []
    for y in range(4):
        for core in range(2):
            for xh in range(2):
                for z in range(4):
                    heads = y * 2 + core
                    moves.append((index(y, core, xh, z), index(z, xh, heads // 4, heads % 4)))
    return moves


def on_device(query_in, key_in, value_in, out_grads, doc_starts):
    all_tokens = query_in.shape[0] * 8
    xh, z = lax.axis_index("xh"), lax.axis_index("z")
    place = jnp.stack(
        [lax.axis_index(X), lax.axis_index("y"), z, lax.axis_index("core")]
    ).astype(jnp.int32)
    k_own = by_head(key_in)
    k_oth = shifted(k_own, "xh", 1)
    v_own = by_head(value_in)
    v_oth = shifted(v_own, "xh", 1)
    q, g = by_head(query_in), by_head(out_grads)
    attended, near, far = attention(
        doc_starts, xh.astype(jnp.int32)[None], q, g, k_own, k_oth, v_own, v_oth
    )
    value_grads = (near + shifted(far, "xh", 1)).astype(jnp.bfloat16)

    def columns(tile):
        moved = lax.ppermute(tile, ("y", "core", "xh", "z"), column_moves())
        own = ring(moved, "y")
        other = tuple(shifted(p, "core", 1) for p in own)
        return own, other

    own_a, oth_a = columns(attended)
    rows_a = ring(stacked(ring(attended, X)), "z")
    own_g, oth_g = columns(value_grads)
    rows_g = ring(stacked(ring(value_grads, "z")), X)
    input_factor = factor(place, rows_a, own_a, oth_a, False, all_tokens)
    grad_factor = factor(place, rows_g, own_g, oth_g, True, all_tokens)
    return (input_factor, grad_factor)


def solution(mesh):
    split = Mesh(mesh.devices.reshape(4, 2, 2, 4, 2), ("y", "core", "xh", "z", "xl"))
    tokens, features = ("xh", "z"), ("y", "core", "xl")
    spec = P(tokens, features)
    out = P(("y", "core"), ("xh", "z", "xl"))
    return jax.shard_map(
        on_device, mesh=split, in_specs=(spec, spec, spec, spec, P()), out_specs=(out, out),
        check_vma=False,
    )
```

time: 788 us -> 440 us (0.56)
  waiting for transfers between devices: 474 us -> 168 us
  Pallas kernels: 0 us -> 184 us
  blocking collectives: 126 us -> 0 us
  starting transfers between devices: 4.22 us -> 65.5 us
  local copies, waits for them, and re-layouts: 67.7 us -> 14.4 us
  matrix products: 43.8 us -> 0 us
  loops' own time: 24.5 us -> 0 us
  other arithmetic: 26.3 us -> 1.95 us
  between operations: 15.6 us -> 1.28 us
    all_gather x14 -> x0, waiting for transfers between devices: 400 us -> none  [the longest x10 254 us: all_blocks(): tiles = lax.all_gather(tiles, axes[k], axis=0, tiled=True)]
    pallas_call x0 -> x5, Pallas kernels: none -> 184 us  [the longest x2 129 us: stacked(): pl.pallas_call(stack_kernel, out_shape=jax.ShapeDtypeStruct((rows, *parts...]
    ppermute x0 -> x39, waiting for transfers between devices: none -> 140 us  [the longest x37 122 us: shifted(): return lax.ppermute(x, axis, [(i, (i + by) % count) for i in range(count)])]
    all_gather x8 -> x0, blocking collectives: 126 us -> none  [all_blocks(): tiles = lax.all_gather(tiles, axes[k], axis=0, tiled=True)]
    reduce_scatter x2 -> x0, waiting for transfers between devices: 66 us -> none  [from_root(): own = lax.psum_scatter(padded, axis, scatter_dimension=0, tiled=True)]
    ppermute x0 -> x39, starting transfers between devices: none -> 49.8 us  [the longest x37 42.3 us: shifted(): return lax.ppermute(x, axis, [(i, (i + by) % count) for i in range(count)])]
    dot_general x7 -> x0, matrix products: 43.8 us -> none  [the longest x1 17.8 us: update(): jnp.einsum('hqk,qhd->khd', weights, piece_grads, preferred_element_type=j...]
    dot_general x2 -> x0, local copies, waits for them, and re-layouts: 24.8 us -> none  [the longest x1 12.5 us: on_device(): jnp.einsum('acnf,ang->cfg', rows_grads, cols_grads, preferred_element_typ...]
  transfers between devices with their start and end apart: 17 -> 43, of which waited for: 14 -> 17; matrix products, arithmetic and copies ran while one was open for 16% -> 3% of each run, Pallas kernels for 0% -> 32%
where the time goes in v1:
time: 440 us; the launch traced here: 435 us
  Pallas kernels  184 us (42%)
  waiting for transfers between devices  168 us (38%)
  starting transfers between devices  65.5 us (15%)
  local copies, waits for them, and re-layouts  14.4 us (3%)
    pallas_call x2, Pallas kernels, stacked(): pl.pallas_call(stack_kernel, out_shape=jax.ShapeDtypeStruct((rows, *parts...  129 us
    ppermute x37, waiting for transfers between devices, shifted(): return lax.ppermute(x, axis, [(i, (i + by) % count) for i in range(count)])  122 us
    ppermute x37, starting transfers between devices, shifted(): return lax.ppermute(x, axis, [(i, (i + by) % count) for i in range(count)])  42.3 us
    pallas_call x1, Pallas kernels, attention(): pl.pallas_call(attention_kernel, out_shape=(jax.ShapeDtypeStruct((HEAD_DI...  31.9 us
    all_to_all x4, waiting for transfers between devices, by_head(): return lax.all_to_all(x, 'z', split_axis=1, concat_axis=0, tiled=True)  27.5 us
    pallas_call x2, Pallas kernels, factor(): pl.pallas_call(kernel, out_shape=jax.ShapeDtypeStruct((8 * HEAD_DIM, 4 *...  22.6 us
    ppermute x2, waiting for transfers between devices, columns(): moved = lax.ppermute(tile, ('y', 'core', 'xh', 'z'), column_moves())  18.3 us
    all_to_all x4, starting transfers between devices, by_head(): return lax.all_to_all(x, 'z', split_axis=1, concat_axis=0, tiled=True)  15.7 us
  transfers between devices with their start and end apart: 43, of which 17 were waited for; matrix products, arithmetic and copies ran while one was open for 3% of the time, Pallas kernels for 32%

profile of v1, /device:TPU:24, one launch (start us, length us, event | category | flops | bytes accessed | tf_op | source)
XLA Modules:
  0.0 434.7 jit_solution(12325547613452415142)
XLA Ops:
  2.6 5.3 %all-to-all-start.2 = ((bf16[512,4,128]{2,0,1:T(8,128)(2,1)}), bf16[512,4,128]{2,0,1:T(8,128)(2,1)S(1)}, u32[]{:S(2)}, u32[]{:S(2)}) async-start(bf16[512,4,128]{2,0,1:T(8,128)(2,1)} %copy_bitcast_fusion.1), calls=%async_computation.2 | async-start | bytes 1048576 | tf_op jit(solution)/shard_map/all_to_all | solution.py:245
  8.8 8.6 %all-to-all-done.2 = bf16[512,4,128]{2,0,1:T(8,128)(2,1)S(1)} async-done(((bf16[512,4,128]{2,0,1:T(8,128)(2,1)}), bf16[512,4,128]{2,0,1:T(8,128)(2,1)S(1)}, u32[]{:S(2)}, u32[]{:S(2)}) %all-to-all-start.2) | async-done | bytes 524320 | tf_op jit(solution)/shard_map/all_to_all | solution.py:245
  17.3 3.5 all-to-all-start.3
  21.7 7.3 %all-to-all-done.3 = bf16[512,4,128]{2,0,1:T(8,128)(2,1)S(1)} async-done(((bf16[512,4,128]{2,0,1:T(8,128)(2,1)}), bf16[512,4,128]{2,0,1:T(8,128)(2,1)S(1)}, u32[]{:S(2)}, u32[]{:S(2)}) %all-to-all-start.3) | async-done | bytes 524320 | tf_op jit(solution)/shard_map/all_to_all | solution.py:245
  29.1 3.5 all-to-all-start
  37.0 3.5 all-to-all-done
  40.6 3.5 all-to-all-start.1
  44.1 8.0 %all-to-all-done.1 = bf16[512,4,128]{2,0,1:T(8,128)(2,1)S(1)} async-done(((bf16[512,4,128]{2,0,1:T(8,128)(2,1)}), bf16[512,4,128]{2,0,1:T(8,128)(2,1)S(1)}, u32[]{:S(2)}, u32[]{:S(2)}) %all-to-all-start.1) | async-done | bytes 524320 | tf_op jit(solution)/shard_map/all_to_all | solution.py:245
  52.1 4.3 collective-permute-done.1.v_oth
  56.5 31.9 %attention.1 = (bf16[128,2048]{1,0:T(8,128)(2,1)}, f32[128,2048]{1,0:T(8,128)}, f32[128,2048]{1,0:T(8,128)}) custom-call(s32[6]{0:T(128)} %starts.1, s32[1]{0:T(128)} %bitcast.4.where_ref, bf16[2048,128]{1,0:T(8,128)(2,1)} %bitcast.41, bf16[2048,128]{1,0:T(8,128)(2,1)} %bitcast.42, bf16[2048,128]{1,0:T(8,128)(2,1)} %bitcast.38, ...), custom_call_target="tpu_custom_call" | custom-call | tf_op jit(solution)/shard_map/attention/pallas_call | solution.py:119
  92.7 5.6 %collective-permute-start.10 = (bf16[128,2048]{1,0:T(8,128)(2,1)}, bf16[128,2048]{1,0:T(8,128)(2,1)}, u32[]{:S(2)}, u32[]{:S(2)}) collective-permute-start(bf16[128,2048]{1,0:T(8,128)(2,1)} %get-tuple-element.5.refs_0_), channel_id=1, source_target_pairs={{0,0},{2,32},{4,64},{6,96},{8,16},{10,48},{12,80},{14,112},{16,2},... | collective-permute-start | bytes 1572872 | tf_op jit(solution)/shard_map/ppermute | solution.py:279
  98.3 25.4 %collective-permute-done.2.refs_1_ = bf16[128,2048]{1,0:T(8,128)(2,1)S(1)} collective-permute-done((bf16[128,2048]{1,0:T(8,128)(2,1)}, bf16[128,2048]{1,0:T(8,128)(2,1)S(1)}, u32[]{:S(2)}, u32[]{:S(2)}) %collective-permute-start.2) | collective-permute-done | bytes 524320 | tf_op jit(solution)/shard_map/ppermute | solution.py:143
  128.2 18.3 %collective-permute-done.10.refs_6_ = bf16[128,2048]{1,0:T(8,128)(2,1)} collective-permute-done((bf16[128,2048]{1,0:T(8,128)(2,1)}, bf16[128,2048]{1,0:T(8,128)(2,1)}, u32[]{:S(2)}, u32[]{:S(2)}) %collective-permute-start.10) | collective-permute-done | bytes 524320 | tf_op jit(solution)/shard_map/ppermute | solution.py:279
  153.2 64.7 %stack.22.refs_1_ = bf16[512,2048]{1,0:T(8,128)(2,1)} custom-call(bf16[128,2048]{1,0:T(8,128)(2,1)} %get-tuple-element.5.refs_0_, bf16[128,2048]{1,0:T(8,128)(2,1)} %copy-done.10, bf16[128,2048]{1,0:T(8,128)(2,1)} %copy-done.11, bf16[64,2048]{1,0:T(8,128)(2,1)} %copy-done.25, bf16[64,2048]{1,0:T(8,128)(2,1)} %collective-permute-done.5.refs_4_), custom_call_target="tpu_custom_call" | custom-call | tf_op jit(solution)/shard_map/stack/pallas_call | solution.py:170
  233.2 39.3 %collective-permute-done.23.refs_3_ = bf16[64,2048]{1,0:T(8,128)(2,1)S(1)} collective-permute-done((bf16[64,2048]{1,0:T(8,128)(2,1)S(1)}, bf16[64,2048]{1,0:T(8,128)(2,1)S(1)}, u32[]{:S(2)}, u32[]{:S(2)}) %collective-permute-start.23) | collective-permute-done | bytes 262176 | tf_op jit(solution)/shard_map/ppermute | solution.py:143
  275.5 64.7 %stack.23.refs_1_ = bf16[512,2048]{1,0:T(8,128)(2,1)} custom-call(bf16[128,2048]{1,0:T(8,128)(2,1)} %copy-done.8, bf16[128,2048]{1,0:T(8,128)(2,1)} %collective-permute-done.21.refs_1_, bf16[128,2048]{1,0:T(8,128)(2,1)} %collective-permute-done.22.refs_2_, bf16[64,2048]{1,0:T(8,128)(2,1)} %copy-done.26, bf16[64,2048]{1,0:T(8,128)(2,1)} %copy-done.27), custom_call_target="tpu_custom_call" | custom-call | tf_op jit(solution)/shard_map/stack/pallas_call | solution.py:170
  343.9 13.6 %collective-permute-done.30.refs_7_ = bf16[128,2048]{1,0:T(8,128)(2,1)S(1)} collective-permute-done((bf16[128,2048]{1,0:T(8,128)(2,1)}, bf16[128,2048]{1,0:T(8,128)(2,1)S(1)}, u32[]{:S(2)}, u32[]{:S(2)}) %collective-permute-start.30) | collective-permute-done | bytes 524320 | tf_op jit(solution)/shard_map/ppermute | solution.py:143
  361.0 11.5 %collective-permute-done.31.refs_8_ = bf16[128,2048]{1,0:T(8,128)(2,1)} collective-permute-done((bf16[128,2048]{1,0:T(8,128)(2,1)}, bf16[128,2048]{1,0:T(8,128)(2,1)}, u32[]{:S(2)}, u32[]{:S(2)}) %collective-permute-start.31) | collective-permute-done | bytes 524320 | tf_op jit(solution)/shard_map/ppermute | solution.py:143
  378.2 3.9 collective-permute-start.9
  382.1 7.7 %collective-permute-done.25.refs_2_ = bf16[512,2048]{1,0:T(8,128)(2,1)S(1)} collective-permute-done((bf16[512,2048]{1,0:T(8,128)(2,1)}, bf16[512,2048]{1,0:T(8,128)(2,1)S(1)}, u32[]{:S(2)}, u32[]{:S(2)}) %collective-permute-start.25) | collective-permute-done | bytes 2097184 | tf_op jit(solution)/shard_map/ppermute | solution.py:143
  393.4 5.6 %collective-permute-done.33.refs_10_ = bf16[64,2048]{1,0:T(8,128)(2,1)} collective-permute-done((bf16[64,2048]{1,0:T(8,128)(2,1)S(1)}, bf16[64,2048]{1,0:T(8,128)(2,1)}, u32[]{:S(2)}, u32[]{:S(2)}) %collective-permute-start.33) | collective-permute-done | bytes 262176 | tf_op jit(solution)/shard_map/ppermute | solution.py:143
  399.1 6.3 %collective-permute-done.8.refs_4_ = bf16[256,2048]{1,0:T(8,128)(2,1)S(1)} collective-permute-done((bf16[256,2048]{1,0:T(8,128)(2,1)S(1)}, bf16[256,2048]{1,0:T(8,128)(2,1)S(1)}, u32[]{:S(2)}, u32[]{:S(2)}) %collective-permute-start.8) | collective-permute-done | bytes 1048608 | tf_op jit(solution)/shard_map/ppermute | solution.py:143
  406.7 11.3 %factor_x_first.1 = f32[1024,512]{1,0:T(8,128)} custom-call(s32[4]{0:T(128)} %pad_add_fusion.refs_0_, bf16[512,2048]{1,0:T(8,128)(2,1)} %stack.22.refs_1_, bf16[512,2048]{1,0:T(8,128)(2,1)} %copy-done.1, bf16[512,2048]{1,0:T(8,128)(2,1)} %collective-permute-done.7.refs_3_, bf16[256,2048]{1,0:T(8,128)(2,1)} %copy-done.12, ...), custom_call_target="tpu_custom_call" | custom-call | tf_op jit(solution)/shard_map/factor_x_first/pallas_call | solution.py:229
  423.2 11.3 %factor_z_first.1 = f32[1024,512]{1,0:T(8,128)} custom-call(s32[4]{0:T(128)} %pad_add_fusion.refs_0_, bf16[512,2048]{1,0:T(8,128)(2,1)} %stack.23.refs_1_, bf16[512,2048]{1,0:T(8,128)(2,1)} %copy-done.2, bf16[512,2048]{1,0:T(8,128)(2,1)} %copy-done.3, bf16[256,2048]{1,0:T(8,128)(2,1)} %copy-done.13, bf16[256,2048]{1,0:T(8,128)(2,1)} %collective-permute-done.28.refs_5_, ...), custom_call_target="tpu_custom_call" | custom-call | tf_op jit(solution)/shard_map/factor_z_first/pallas_call | solution.py:229
  (141 shorter events, 64.6 us)
Async XLA Ops:
  88.4 60.1 %collective-permute-start.20 = (f32[128,2048]{1,0:T(8,128)}, f32[128,2048]{1,0:T(8,128)S(1)}, u32[]{:S(2)}, u32[]{:S(2)}) collective-permute-start(f32[128,2048]{1,0:T(8,128)} %get-tuple-element.7), channel_id=1, source_target_pairs={{0,8},{8,0},{1,9},{9,1},{2,10},{10,2},{3,11},{11,3},{4,12},{12,4},... | collective-permute-start | bytes 3145736 | tf_op jit(solution)/shard_map/ppermute | solution.py:143
  88.5 35.2 %collective-permute-start.2 = (bf16[128,2048]{1,0:T(8,128)(2,1)}, bf16[128,2048]{1,0:T(8,128)(2,1)S(1)}, u32[]{:S(2)}, u32[]{:S(2)}) collective-permute-start(bf16[128,2048]{1,0:T(8,128)(2,1)} %get-tuple-element.5.refs_0_), channel_id=1, source_target_pairs={{0,1},{1,8},{8,9},{9,0},{2,3},{3,10},{10,11},{11,2},{4,5},{5,12},{... | collective-permute-start | bytes 1572872 | tf_op jit(solution)/shard_map/ppermute | solution.py:143
  90.1 36.1 %collective-permute-start.3 = (bf16[128,2048]{1,0:T(8,128)(2,1)}, bf16[128,2048]{1,0:T(8,128)(2,1)S(1)}, u32[]{:S(2)}, u32[]{:S(2)}) collective-permute-start(bf16[128,2048]{1,0:T(8,128)(2,1)} %get-tuple-element.5.refs_0_), channel_id=1, source_target_pairs={{0,9},{1,0},{8,1},{9,8},{2,11},{3,2},{10,3},{11,10},{4,13},{5,4},{... | collective-permute-start | bytes 1572872 | tf_op jit(solution)/shard_map/ppermute | solution.py:143
  92.7 53.9 %collective-permute-start.10 = (bf16[128,2048]{1,0:T(8,128)(2,1)}, bf16[128,2048]{1,0:T(8,128)(2,1)}, u32[]{:S(2)}, u32[]{:S(2)}) collective-permute-start(bf16[128,2048]{1,0:T(8,128)(2,1)} %get-tuple-element.5.refs_0_), channel_id=1, source_target_pairs={{0,0},{2,32},{4,64},{6,96},{8,16},{10,48},{12,80},{14,112},{16,2},... | collective-permute-start | bytes 1572872 | tf_op jit(solution)/shard_map/ppermute | solution.py:279
  123.7 26.2 %collective-permute-start.4 = (bf16[64,2048]{1,0:T(8,128)(2,1)S(1)}, bf16[64,2048]{1,0:T(8,128)(2,1)S(1)}, u32[]{:S(2)}, u32[]{:S(2)}) collective-permute-start(bf16[64,2048]{1,0:T(8,128)(2,1)S(1)} %slice.48), channel_id=1, source_target_pairs={{0,1},{1,8},{8,9},{9,0},{2,3},{3,10},{10,11},{11,2},{4,5},{5,12},{... | collective-permute-start | bytes 786440 | tf_op jit(solution)/shard_map/ppermute | solution.py:143
  126.2 24.7 %collective-permute-start.5 = (bf16[64,2048]{1,0:T(8,128)(2,1)S(1)}, bf16[64,2048]{1,0:T(8,128)(2,1)}, u32[]{:S(2)}, u32[]{:S(2)}) collective-permute-start(bf16[64,2048]{1,0:T(8,128)(2,1)S(1)} %slice.49), channel_id=1, source_target_pairs={{0,9},{1,0},{8,1},{9,8},{2,11},{3,2},{10,3},{11,10},{4,13},{5,4},{... | collective-permute-start | bytes 786440 | tf_op jit(solution)/shard_map/ppermute | solution.py:143
  146.5 71.4 %collective-permute-start.11 = (bf16[128,2048]{1,0:T(8,128)(2,1)}, bf16[128,2048]{1,0:T(8,128)(2,1)}, u32[]{:S(2)}, u32[]{:S(2)}) collective-permute-start(bf16[128,2048]{1,0:T(8,128)(2,1)} %collective-permute-done.10.refs_6_), channel_id=1, source_target_pairs={{0,32},{32,64},{64,96},{96,0},{1,33},{33,65},{65,97},{97,1},{2,34}... | collective-permute-start | bytes 1572872 | tf_op jit(solution)/shard_map/ppermute | solution.py:143
  146.5 72.5 %collective-permute-start.12 = (bf16[128,2048]{1,0:T(8,128)(2,1)}, bf16[128,2048]{1,0:T(8,128)(2,1)}, u32[]{:S(2)}, u32[]{:S(2)}) collective-permute-start(bf16[128,2048]{1,0:T(8,128)(2,1)} %collective-permute-done.10.refs_6_), channel_id=1, source_target_pairs={{0,96},{32,0},{64,32},{96,64},{1,97},{33,1},{65,33},{97,65},{2,98}... | collective-permute-start | bytes 1572872 | tf_op jit(solution)/shard_map/ppermute | solution.py:143
  148.6 72.7 %collective-permute-start.15 = (bf16[128,2048]{1,0:T(8,128)(2,1)}, bf16[128,2048]{1,0:T(8,128)(2,1)}, u32[]{:S(2)}, u32[]{:S(2)}) collective-permute-start(bf16[128,2048]{1,0:T(8,128)(2,1)} %collective-permute-done.10.refs_6_), channel_id=1, source_target_pairs={{0,16},{16,0},{1,17},{17,1},{2,18},{18,2},{3,19},{19,3},{4,20},{20... | collective-permute-start | bytes 1572872 | tf_op jit(solution)/shard_map/ppermute | solution.py:143
  149.9 74.6 %collective-permute-start.21 = (bf16[128,2048]{1,0:T(8,128)(2,1)S(1)}, bf16[128,2048]{1,0:T(8,128)(2,1)}, u32[]{:S(2)}, u32[]{:S(2)}) collective-permute-start(bf16[128,2048]{1,0:T(8,128)(2,1)S(1)} %add_convert_fusion.refs_0_), channel_id=1, source_target_pairs={{0,2},{2,4},{4,6},{6,0},{1,3},{3,5},{5,7},{7,1},{8,10},{10,12},{12... | collective-permute-start | bytes 1572872 | tf_op jit(solution)/shard_map/ppermute | solution.py:143
  150.9 75.4 %collective-permute-start.22 = (bf16[128,2048]{1,0:T(8,128)(2,1)S(1)}, bf16[128,2048]{1,0:T(8,128)(2,1)}, u32[]{:S(2)}, u32[]{:S(2)}) collective-permute-start(bf16[128,2048]{1,0:T(8,128)(2,1)S(1)} %add_convert_fusion.refs_0_), channel_id=1, source_target_pairs={{0,6},{2,0},{4,2},{6,4},{1,7},{3,1},{5,3},{7,5},{8,14},{10,8},{12,... | collective-permute-start | bytes 1572872 | tf_op jit(solution)/shard_map/ppermute | solution.py:143
  217.9 154.5 %collective-permute-start.6 = (bf16[512,2048]{1,0:T(8,128)(2,1)}, bf16[512,2048]{1,0:T(8,128)(2,1)S(1)}, u32[]{:S(2)}, u32[]{:S(2)}) collective-permute-start(bf16[512,2048]{1,0:T(8,128)(2,1)} %stack.22.refs_1_), channel_id=1, source_target_pairs={{0,2},{2,4},{4,6},{6,0},{1,3},{3,5},{5,7},{7,1},{8,10},{10,12},{12... | collective-permute-start | bytes 6291464 | tf_op jit(solution)/shard_map/ppermute | solution.py:143
  221.3 151.7 %collective-permute-start.7 = (bf16[512,2048]{1,0:T(8,128)(2,1)}, bf16[512,2048]{1,0:T(8,128)(2,1)}, u32[]{:S(2)}, u32[]{:S(2)}) collective-permute-start(bf16[512,2048]{1,0:T(8,128)(2,1)} %stack.22.refs_1_), channel_id=1, source_target_pairs={{0,6},{2,0},{4,2},{6,4},{1,7},{3,1},{5,3},{7,5},{8,14},{10,8},{12,... | collective-permute-start | bytes 6291464 | tf_op jit(solution)/shard_map/ppermute | solution.py:143
  226.4 46.2 %collective-permute-start.23 = (bf16[64,2048]{1,0:T(8,128)(2,1)S(1)}, bf16[64,2048]{1,0:T(8,128)(2,1)S(1)}, u32[]{:S(2)}, u32[]{:S(2)}) collective-permute-start(bf16[64,2048]{1,0:T(8,128)(2,1)S(1)} %slice.54), channel_id=1, source_target_pairs={{0,2},{2,4},{4,6},{6,0},{1,3},{3,5},{5,7},{7,1},{8,10},{10,12},{12... | collective-permute-start | bytes 786440 | tf_op jit(solution)/shard_map/ppermute | solution.py:143
  227.4 47.4 %collective-permute-start.24 = (bf16[64,2048]{1,0:T(8,128)(2,1)S(1)}, bf16[64,2048]{1,0:T(8,128)(2,1)S(1)}, u32[]{:S(2)}, u32[]{:S(2)}) collective-permute-start(bf16[64,2048]{1,0:T(8,128)(2,1)S(1)} %slice.55), channel_id=1, source_target_pairs={{0,6},{2,0},{4,2},{6,4},{1,7},{3,1},{5,3},{7,5},{8,14},{10,8},{12,... | collective-permute-start | bytes 786440 | tf_op jit(solution)/shard_map/ppermute | solution.py:143
  233.2 107.0 %collective-permute-start.18 = (bf16[64,2048]{1,0:T(8,128)(2,1)S(1)}, bf16[64,2048]{1,0:T(8,128)(2,1)}, u32[]{:S(2)}, u32[]{:S(2)}) collective-permute-start(bf16[64,2048]{1,0:T(8,128)(2,1)S(1)} %collective-permute-done.13.refs_9_), channel_id=1, source_target_pairs={{0,16},{16,0},{1,17},{17,1},{2,18},{18,2},{3,19},{19,3},{4,20},{20... | collective-permute-start | bytes 786440 | tf_op jit(solution)/shard_map/ppermute | solution.py:143
  272.5 71.0 %collective-permute-start.29 = (bf16[128,2048]{1,0:T(8,128)(2,1)S(1)}, bf16[128,2048]{1,0:T(8,128)(2,1)}, u32[]{:S(2)}, u32[]{:S(2)}) collective-permute-start(bf16[128,2048]{1,0:T(8,128)(2,1)S(1)} %add_convert_fusion.refs_0_), channel_id=1, source_target_pairs={{0,0},{2,32},{4,64},{6,96},{8,16},{10,48},{12,80},{14,112},{16,2},... | collective-permute-start | bytes 1572872 | tf_op jit(solution)/shard_map/ppermute | solution.py:279
  275.5 64.8 %collective-permute-start.19 = (bf16[64,2048]{1,0:T(8,128)(2,1)}, bf16[64,2048]{1,0:T(8,128)(2,1)}, u32[]{:S(2)}, u32[]{:S(2)}) collective-permute-start(bf16[64,2048]{1,0:T(8,128)(2,1)} %collective-permute-done.14.refs_10_), channel_id=1, source_target_pairs={{0,16},{16,0},{1,17},{17,1},{2,18},{18,2},{3,19},{19,3},{4,20},{20... | collective-permute-start | bytes 786440 | tf_op jit(solution)/shard_map/ppermute | solution.py:143
  340.2 49.5 %collective-permute-start.25 = (bf16[512,2048]{1,0:T(8,128)(2,1)}, bf16[512,2048]{1,0:T(8,128)(2,1)S(1)}, u32[]{:S(2)}, u32[]{:S(2)}) collective-permute-start(bf16[512,2048]{1,0:T(8,128)(2,1)} %stack.23.refs_1_), channel_id=1, source_target_pairs={{0,1},{1,8},{8,9},{9,0},{2,3},{3,10},{10,11},{11,2},{4,5},{5,12},{... | collective-permute-start | bytes 6291464 | tf_op jit(solution)/shard_map/ppermute | solution.py:143
  340.3 51.3 %collective-permute-start.26 = (bf16[512,2048]{1,0:T(8,128)(2,1)}, bf16[512,2048]{1,0:T(8,128)(2,1)S(1)}, u32[]{:S(2)}, u32[]{:S(2)}) collective-permute-start(bf16[512,2048]{1,0:T(8,128)(2,1)} %stack.23.refs_1_), channel_id=1, source_target_pairs={{0,9},{1,0},{8,1},{9,8},{2,11},{3,2},{10,3},{11,10},{4,13},{5,4},{... | collective-permute-start | bytes 6291464 | tf_op jit(solution)/shard_map/ppermute | solution.py:143
  378.1 27.3 %collective-permute-start.8 = (bf16[256,2048]{1,0:T(8,128)(2,1)S(1)}, bf16[256,2048]{1,0:T(8,128)(2,1)S(1)}, u32[]{:S(2)}, u32[]{:S(2)}) collective-permute-start(bf16[256,2048]{1,0:T(8,128)(2,1)S(1)} %slice.50), channel_id=1, source_target_pairs={{0,2},{2,4},{4,6},{6,0},{1,3},{3,5},{5,7},{7,1},{8,10},{10,12},{12... | collective-permute-start | bytes 3145736 | tf_op jit(solution)/shard_map/ppermute | solution.py:143
  378.2 27.3 %collective-permute-start.9 = (bf16[256,2048]{1,0:T(8,128)(2,1)S(1)}, bf16[256,2048]{1,0:T(8,128)(2,1)}, u32[]{:S(2)}, u32[]{:S(2)}) collective-permute-start(bf16[256,2048]{1,0:T(8,128)(2,1)S(1)} %slice.51), channel_id=1, source_target_pairs={{0,6},{2,0},{4,2},{6,4},{1,7},{3,1},{5,3},{7,5},{8,14},{10,8},{12,... | collective-permute-start | bytes 3145736 | tf_op jit(solution)/shard_map/ppermute | solution.py:143
  393.4 26.4 %collective-permute-start.27 = (bf16[256,2048]{1,0:T(8,128)(2,1)}, bf16[256,2048]{1,0:T(8,128)(2,1)S(1)}, u32[]{:S(2)}, u32[]{:S(2)}) collective-permute-start(bf16[256,2048]{1,0:T(8,128)(2,1)} %slice.56), channel_id=1, source_target_pairs={{0,1},{1,8},{8,9},{9,0},{2,3},{3,10},{10,11},{11,2},{4,5},{5,12},{... | collective-permute-start | bytes 3145736 | tf_op jit(solution)/shard_map/ppermute | solution.py:143
  399.0 24.2 %collective-permute-start.28 = (bf16[256,2048]{1,0:T(8,128)(2,1)}, bf16[256,2048]{1,0:T(8,128)(2,1)}, u32[]{:S(2)}, u32[]{:S(2)}) collective-permute-start(bf16[256,2048]{1,0:T(8,128)(2,1)} %slice.57), channel_id=1, source_target_pairs={{0,9},{1,0},{8,1},{9,8},{2,11},{3,2},{10,3},{11,10},{4,13},{5,4},{... | collective-permute-start | bytes 3145736 | tf_op jit(solution)/shard_map/ppermute | solution.py:143
  (47 other events, 855.0 us)

commit v2 on v1

--- a/solution.py
+++ b/solution.py
@@ -1,3 +1,4 @@
+import functools
 import math
 
 import jax
@@ -12,7 +13,7 @@
 X = ("xh", "xl")
 MASK_FLOOR = -1e30
 KEY_STEP = 512
-QUERY_STEP = 256
+QUERY_STEP = 512
 VMEM_BYTES = 56 * 1024 * 1024
 
 
@@ -50,34 +51,42 @@
         pos = first + lax.broadcasted_iota(jnp.int32, (1, QUERY_STEP), 1)
         begin = jnp.zeros((1, QUERY_STEP), jnp.int32)
         finish = jnp.full((1, QUERY_STEP), all_tokens, jnp.int32)
-        lowest = jnp.int32(0)
-        highest = jnp.int32(all_tokens)
+        lowest, latest = jnp.int32(0), jnp.int32(0)
+        highest, soonest = jnp.int32(all_tokens), jnp.int32(all_tokens)
         for d in range(docs):
             start = starts[d]
             lowest = jnp.where(start <= first, jnp.maximum(lowest, start), lowest)
             highest = jnp.where(start > last, jnp.minimum(highest, start), highest)
+            latest = jnp.where(start <= last, jnp.maximum(latest, start), latest)
+            soonest = jnp.where(start > first, jnp.minimum(soonest, start), soonest)
             begin = jnp.where(start <= pos, jnp.maximum(begin, start), begin)
             finish = jnp.where(start > pos, jnp.minimum(finish, start), finish)
         step_from = lowest // KEY_STEP
         step_to = (highest + KEY_STEP - 1) // KEY_STEP
+        inside_from = jnp.minimum((latest + KEY_STEP - 1) // KEY_STEP, step_to)
+        inside_to = jnp.maximum(soonest // KEY_STEP, inside_from)
         queries = q_ref[pl.ds(row, QUERY_STEP), :]
         cotangents = g_ref[pl.ds(row, QUERY_STEP), :]
         key_iota = lax.broadcasted_iota(jnp.int32, (KEY_STEP, QUERY_STEP), 0)
 
-        def score_step(step, peak):
+        def score_step(step, peak, masked):
             at = pl.multiple_of(step * KEY_STEP, KEY_STEP)
             s = lax.dot_general(
                 k_all[pl.ds(at, KEY_STEP), :], queries, (((1,), (1,)), ((), ())),
                 preferred_element_type=jnp.float32,
             ) * scale
-            allowed = (key_iota >= begin - at) & (key_iota < finish - at)
-            s = jnp.where(allowed, s, MASK_FLOOR)
+            if masked:
+                allowed = (key_iota >= begin - at) & (key_iota < finish - at)
+                s = jnp.where(allowed, s, MASK_FLOOR)
             scores[pl.ds(at, KEY_STEP), :] = s
             return jnp.maximum(peak, jnp.max(s.reshape(groups, 8, QUERY_STEP), axis=0))
 
-        peak = lax.fori_loop(
-            step_from, step_to, score_step, jnp.full((8, QUERY_STEP), MASK_FLOOR, jnp.float32)
-        )
+        edge_step = functools.partial(score_step, masked=True)
+        inside_step = functools.partial(score_step, masked=False)
+        peak = jnp.full((8, QUERY_STEP), MASK_FLOOR, jnp.float32)
+        peak = lax.fori_loop(step_from, inside_from, edge_step, peak)
+        peak = lax.fori_loop(inside_from, inside_to, inside_step, peak)
+        peak = lax.fori_loop(inside_to, step_to, edge_step, peak)
         peak = jnp.max(peak, axis=0, keepdims=True)
 
         def mass_step(step, mass):
@@ -108,7 +117,7 @@
     lax.fori_loop(0, half // QUERY_STEP, query_block, 0)
     for at in range(0, half, KEY_STEP):
         near_ref[:, at : at + KEY_STEP] = grads[pl.ds(own_at + at, KEY_STEP), :].T
-        far_ref[:, at : at + KEY_STEP] = grads[pl.ds(oth_at + at, KEY_STEP), :].T
+        far_ref[:, at : at + KEY_STEP] = grads[pl.ds(oth_at + at, KEY_STEP), :].T.astype(jnp.bfloat16)
 
 
 def attention(starts, half_id, q, g, k_own, k_oth, v_own, v_oth):
@@ -121,7 +130,7 @@
         out_shape=(
             jax.ShapeDtypeStruct((HEAD_DIM, half), jnp.bfloat16),
             jax.ShapeDtypeStruct((HEAD_DIM, half), jnp.float32),
-            jax.ShapeDtypeStruct((HEAD_DIM, half), jnp.float32),
+            jax.ShapeDtypeStruct((HEAD_DIM, half), jnp.bfloat16),
         ),
         in_specs=[smem, smem, vmem, vmem, hbm, hbm, hbm, hbm],
         out_specs=(vmem, vmem, vmem),
@@ -143,46 +152,44 @@
     return lax.ppermute(x, axis, [(i, (i + by) % count) for i in range(count)])
 
 
+def near_ring(x, axis):
+    return shifted(x, axis, 1), shifted(x, axis, -1)
+
+
+def far_ring(below, above, axis):
+    half = below.shape[0] // 2
+    return shifted(below[:half], axis, 1), shifted(above[half:], axis, -1)
+
+
 def ring(x, axis):
-    half = x.shape[0] // 2
-    below, above = shifted(x, axis, 1), shifted(x, axis, -1)
-    far = (shifted(below[:half], axis, 1), shifted(above[half:], axis, -1))
-    return (x, below, above, *far)
+    below, above = near_ring(x, axis)
+    return (x, below, above, *far_ring(below, above, axis))
 
 
 def stack_kernel(*refs):
-    count = len(refs) - 2
-    parts, out, sems = refs[:count], refs[count], refs[count + 1]
-    copies, at = [], 0
-    for k, part in enumerate(parts):
-        rows = part.shape[0]
-        copies.append(pltpu.make_async_copy(part, out.at[pl.ds(at, rows)], sems.at[k]))
-        at += rows
-    for copy in copies:
-        copy.start()
-    for copy in copies:
-        copy.wait()
+    out, at = refs[-1], 0
+    for part in refs[:-1]:
+        out[at : at + part.shape[0], :] = part[...]
+        at += part.shape[0]
 
 
 def stacked(parts):
     rows = sum(p.shape[0] for p in parts)
-    hbm = pl.BlockSpec(memory_space=pl.ANY)
+    vmem = pl.BlockSpec(memory_space=pltpu.VMEM)
     return pl.pallas_call(
         stack_kernel,
         out_shape=jax.ShapeDtypeStruct((rows, *parts[0].shape[1:]), parts[0].dtype),
-        in_specs=[hbm] * len(parts),
-        out_specs=hbm,
-        scratch_shapes=[pltpu.SemaphoreType.DMA((len(parts),))],
+        in_specs=[vmem] * len(parts),
+        out_specs=vmem,
         name="stack",
     )(*parts)
 
 
-def factor_kernel(place, *refs, z_first, count):
-    row_refs, own_cols, oth_cols = refs[:5], refs[5:10], refs[10:15]
-    out, rows, cols, sems = refs[15], refs[16], refs[17], refs[18]
-    x, y, z, core = place[0], place[1], place[2], place[3]
+def factor_kernel(place, *refs, which, count):
+    z_first = which == 0
+    row_refs, (col_ref, out, rows, cols, sems) = refs[:5], refs[5:]
+    x, z = place[0], place[1]
     block = HEAD_DIM
-    half = block // 2
     copies = []
 
     def start(src, dst):
@@ -191,14 +198,10 @@
         copies.append(copy)
 
     ring_steps = (0, 3, 1, 2)
-    for who, parts in ((core, own_cols), (1 - core, oth_cols)):
-        for k in range(5):
-            if k < 3:
-                at = pl.multiple_of(((y + ring_steps[k]) % 4) * block, block)
-                start(parts[k], cols.at[who, pl.ds(at, block)])
-            else:
-                at = pl.multiple_of(((y + 2) % 4) * block + (k - 3) * half, half)
-                start(parts[k], cols.at[who, pl.ds(at, half)])
+    line = 4 - (x // 2) * 2 - z // 2
+    for n in range(8):
+        at = ((n // 2 + line) % 4) * block
+        start(col_ref.at[pl.ds(n * block, block)], cols.at[n % 2, pl.ds(pl.multiple_of(at, block), block)])
     for k in range(5):
         outer = ring_steps[min(k, 3)]
         inners = ((0, 1, 2, 3), (0, 1, 2, 3), (0, 1, 2, 3), (0, 1), (2, 3))[k]
@@ -222,23 +225,23 @@
         out[at : at + step, :] = total * (1.0 / count)
 
 
-def factor(place, rows, own_cols, oth_cols, z_first, count):
-    tokens = own_cols[0].shape[1]
+def factor(place, rows, cols, which, count):
+    tokens = cols.shape[1]
     hbm = pl.BlockSpec(memory_space=pl.ANY)
-    kernel = lambda *refs: factor_kernel(*refs, z_first=z_first, count=count)
+    kernel = lambda *refs: factor_kernel(*refs, which=which, count=count)
     return pl.pallas_call(
         kernel,
         out_shape=jax.ShapeDtypeStruct((8 * HEAD_DIM, 4 * HEAD_DIM), jnp.float32),
-        in_specs=[pl.BlockSpec(memory_space=pltpu.SMEM)] + [hbm] * 15,
+        in_specs=[pl.BlockSpec(memory_space=pltpu.SMEM)] + [hbm] * 6,
         out_specs=pl.BlockSpec(memory_space=pltpu.VMEM),
         scratch_shapes=[
             pltpu.VMEM((2, 8 * HEAD_DIM, tokens), jnp.bfloat16),
             pltpu.VMEM((2, 4 * HEAD_DIM, tokens), jnp.bfloat16),
-            pltpu.SemaphoreType.DMA((26,)),
+            pltpu.SemaphoreType.DMA((24,)),
         ],
         compiler_params=pltpu.CompilerParams(vmem_limit_bytes=VMEM_BYTES),
-        name="factor_z_first" if z_first else "factor_x_first",
-    )(place, *rows, *own_cols, *oth_cols)
+        name="grad_factor" if which else "input_factor",
+    )(place, *rows, cols)
 
 
 def by_head(x):
@@ -246,25 +249,20 @@
 
 
 def column_moves():
-    def index(y, core, xh, z):
-        return ((y * 2 + core) * 2 + xh) * 4 + z
-
-    moves = []
-    for y in range(4):
-        for core in range(2):
-            for xh in range(2):
-                for z in range(4):
-                    heads = y * 2 + core
-                    moves.append((index(y, core, xh, z), index(z, xh, heads // 4, heads % 4)))
-    return moves
+    ranks = [(y, core, xh, z) for y in range(4) for core in range(2) for xh in range(2) for z in range(4)]
+    place = {rank: n for n, rank in enumerate(ranks)}
+    along_y, in_plane = [], []
+    for y, core, xh, z in ranks:
+        spread = (y + z) % 4
+        along_y.append((place[y, core, xh, z], place[spread, core, xh, z]))
+        in_plane.append((place[spread, core, xh, z], place[spread, xh, y // 2, (y % 2) * 2 + core]))
+    return along_y, in_plane
 
 
 def on_device(query_in, key_in, value_in, out_grads, doc_starts):
     all_tokens = query_in.shape[0] * 8
     xh, z = lax.axis_index("xh"), lax.axis_index("z")
-    place = jnp.stack(
-        [lax.axis_index(X), lax.axis_index("y"), z, lax.axis_index("core")]
-    ).astype(jnp.int32)
+    place = jnp.stack([lax.axis_index(X), z]).astype(jnp.int32)
     k_own = by_head(key_in)
     k_oth = shifted(k_own, "xh", 1)
     v_own = by_head(value_in)
@@ -273,20 +271,30 @@
     attended, near, far = attention(
         doc_starts, xh.astype(jnp.int32)[None], q, g, k_own, k_oth, v_own, v_oth
     )
-    value_grads = (near + shifted(far, "xh", 1)).astype(jnp.bfloat16)
-
-    def columns(tile):
-        moved = lax.ppermute(tile, ("y", "core", "xh", "z"), column_moves())
-        own = ring(moved, "y")
-        other = tuple(shifted(p, "core", 1) for p in own)
-        return own, other
-
-    own_a, oth_a = columns(attended)
-    rows_a = ring(stacked(ring(attended, X)), "z")
-    own_g, oth_g = columns(value_grads)
-    rows_g = ring(stacked(ring(value_grads, "z")), X)
-    input_factor = factor(place, rows_a, own_a, oth_a, False, all_tokens)
-    grad_factor = factor(place, rows_g, own_g, oth_g, True, all_tokens)
+    line = ("y", "core", "xh", "z")
+    along_y, in_plane = column_moves()
+    far = shifted(far, "xh", 1)
+    a_near = near_ring(attended, "z")
+    a_col = lax.ppermute(attended, line, along_y)
+    near, far, attended, a_near, a_col = lax.optimization_barrier((near, far, attended, a_near, a_col))
+    value_grads = (near + far).astype(jnp.bfloat16)
+    g_near = near_ring(value_grads, X)
+    g_col = lax.ppermute(value_grads, line, along_y)
+    a_far = far_ring(*a_near, "z")
+    a_col = lax.ppermute(a_col, line, in_plane)
+    a_near, a_far, a_col, value_grads, g_near, g_col = lax.optimization_barrier(
+        (a_near, a_far, a_col, value_grads, g_near, g_col)
+    )
+    group_a = stacked((attended, *a_near, *a_far))
+    g_far = far_ring(*g_near, X)
+    g_col = lax.ppermute(g_col, line, in_plane)
+    group_g = stacked((value_grads, *g_near, *g_far))
+    cols_a = lax.all_gather(a_col, ("y", "core"), axis=0, tiled=True)
+    cols_g = lax.all_gather(g_col, ("y", "core"), axis=0, tiled=True)
+    rows_a = ring(group_a, X)
+    rows_g = ring(group_g, "z")
+    input_factor = factor(place, rows_a, cols_a, 0, all_tokens)
+    grad_factor = factor(place, rows_g, cols_g, 1, all_tokens)
     return (input_factor, grad_factor)
 
 

time: 440 us -> 269 us (0.61)
  Pallas kernels: 184 us -> 45.2 us
  waiting for transfers between devices: 168 us -> 122 us
  between operations: 1.28 us -> 14.3 us
    pallas_call x2, Pallas kernels: 129 us -> 6.01 us  [stacked(): pl.pallas_call(stack_kernel, out_shape=jax.ShapeDtypeStruct((rows, *parts...]
    ppermute x37 -> x19, waiting for transfers between devices: 122 us -> 78.7 us  [shifted(): return lax.ppermute(x, axis, [(i, (i + by) % count) for i in range(count)])]
    pallas_call x1, Pallas kernels: 31.9 us -> 16.5 us  [attention(): pl.pallas_call(attention_kernel, out_shape=(jax.ShapeDtypeStruct((HEAD_DI...]
    ppermute x2 -> x4, starting transfers between devices: 7.5 us -> 10.4 us  [the longest x1 5.35 us: on_device(): a_col = lax.ppermute(a_col, line, in_plane)]
    ppermute x2 -> x4, waiting for transfers between devices: 18.3 us -> 15.9 us  [the longest x1 15.9 us: on_device(): g_col = lax.ppermute(g_col, line, in_plane)]
    ppermute x37 -> x19, starting transfers between devices: 42.3 us -> 42.1 us  [shifted(): return lax.ppermute(x, axis, [(i, (i + by) % count) for i in range(count)])]
  transfers between devices with their start and end apart: 43 -> 29, of which waited for: 17 -> 16; matrix products, arithmetic and copies ran while one was open for 3% -> 4% of each run, Pallas kernels for 32% -> 7%
where the time goes in v2:
time: 269 us; the launch traced here: 265 us
  waiting for transfers between devices  122 us (45%)
  starting transfers between devices  68.4 us (25%)
  Pallas kernels  45.2 us (17%)
  between operations  14.3 us (5%)
  local copies, waits for them, and re-layouts  13 us (5%)
    ppermute x19, waiting for transfers between devices, shifted(): return lax.ppermute(x, axis, [(i, (i + by) % count) for i in range(count)])  78.7 us
    ppermute x19, starting transfers between devices, shifted(): return lax.ppermute(x, axis, [(i, (i + by) % count) for i in range(count)])  42.1 us
    all_to_all x4, waiting for transfers between devices, by_head(): return lax.all_to_all(x, 'z', split_axis=1, concat_axis=0, tiled=True)  27.5 us
    pallas_call x2, Pallas kernels, factor(): pl.pallas_call(kernel, out_shape=jax.ShapeDtypeStruct((8 * HEAD_DIM, 4 *...  22.6 us
    pallas_call x1, Pallas kernels, attention(): pl.pallas_call(attention_kernel, out_shape=(jax.ShapeDtypeStruct((HEAD_DI...  16.5 us
    ppermute x1, waiting for transfers between devices, on_device(): g_col = lax.ppermute(g_col, line, in_plane)  15.9 us
    all_to_all x4, starting transfers between devices, by_head(): return lax.all_to_all(x, 'z', split_axis=1, concat_axis=0, tiled=True)  15.7 us
    slice x8, local copies, waits for them, and re-layouts, far_ring(): return (shifted(below[:half], axis, 1), shifted(above[half:], axis, -1))  6.16 us
  transfers between devices with their start and end apart: 29, of which 16 were waited for; matrix products, arithmetic and copies ran while one was open for 4% of the time, Pallas kernels for 7%

profile of v2, /device:TPU:24, one launch (start us, length us, event | category | flops | bytes accessed | tf_op | source)
XLA Modules:
  0.0 264.8 jit_solution(14071044529279203747)
XLA Ops:
  9.1 5.3 %all-to-all-start.2 = ((bf16[512,4,128]{2,0,1:T(8,128)(2,1)}), bf16[512,4,128]{2,0,1:T(8,128)(2,1)S(1)}, u32[]{:S(2)}, u32[]{:S(2)}) async-start(bf16[512,4,128]{2,0,1:T(8,128)(2,1)} %copy_bitcast_fusion.1), calls=%async_computation.2 | async-start | bytes 1048576 | tf_op jit(solution)/shard_map/all_to_all | solution.py:248
  15.3 8.6 %all-to-all-done.2 = bf16[512,4,128]{2,0,1:T(8,128)(2,1)S(1)} async-done(((bf16[512,4,128]{2,0,1:T(8,128)(2,1)}), bf16[512,4,128]{2,0,1:T(8,128)(2,1)S(1)}, u32[]{:S(2)}, u32[]{:S(2)}) %all-to-all-start.2) | async-done | bytes 524320 | tf_op jit(solution)/shard_map/all_to_all | solution.py:248
  23.9 3.5 %all-to-all-start.3 = ((bf16[512,4,128]{2,0,1:T(8,128)(2,1)}), bf16[512,4,128]{2,0,1:T(8,128)(2,1)S(1)}, u32[]{:S(2)}, u32[]{:S(2)}) async-start(bf16[512,4,128]{2,0,1:T(8,128)(2,1)} %copy_bitcast_fusion), calls=%async_computation.3 | async-start | bytes 1048576 | tf_op jit(solution)/shard_map/all_to_all | solution.py:248
  28.3 7.3 %all-to-all-done.3 = bf16[512,4,128]{2,0,1:T(8,128)(2,1)S(1)} async-done(((bf16[512,4,128]{2,0,1:T(8,128)(2,1)}), bf16[512,4,128]{2,0,1:T(8,128)(2,1)S(1)}, u32[]{:S(2)}, u32[]{:S(2)}) %all-to-all-start.3) | async-done | bytes 524320 | tf_op jit(solution)/shard_map/all_to_all | solution.py:248
  35.6 3.5 %all-to-all-start = ((bf16[512,4,128]{2,0,1:T(8,128)(2,1)}), bf16[512,4,128]{2,0,1:T(8,128)(2,1)S(1)}, u32[]{:S(2)}, u32[]{:S(2)}) async-start(bf16[512,4,128]{2,0,1:T(8,128)(2,1)} %copy_bitcast_fusion.3), calls=%async_computation | async-start | bytes 1048576 | tf_op jit(solution)/shard_map/all_to_all | solution.py:248
  43.6 3.5 %all-to-all-done = bf16[512,4,128]{2,0,1:T(8,128)(2,1)S(1)} async-done(((bf16[512,4,128]{2,0,1:T(8,128)(2,1)}), bf16[512,4,128]{2,0,1:T(8,128)(2,1)S(1)}, u32[]{:S(2)}, u32[]{:S(2)}) %all-to-all-start) | async-done | bytes 524320 | tf_op jit(solution)/shard_map/all_to_all | solution.py:248
  47.1 3.5 %all-to-all-start.1 = ((bf16[512,4,128]{2,0,1:T(8,128)(2,1)}), bf16[512,4,128]{2,0,1:T(8,128)(2,1)S(1)}, u32[]{:S(2)}, u32[]{:S(2)}) async-start(bf16[512,4,128]{2,0,1:T(8,128)(2,1)} %copy_bitcast_fusion.2), calls=%async_computation.1 | async-start | bytes 1048576 | tf_op jit(solution)/shard_map/all_to_all | solution.py:248
  50.7 8.0 %all-to-all-done.1 = bf16[512,4,128]{2,0,1:T(8,128)(2,1)S(1)} async-done(((bf16[512,4,128]{2,0,1:T(8,128)(2,1)}), bf16[512,4,128]{2,0,1:T(8,128)(2,1)S(1)}, u32[]{:S(2)}, u32[]{:S(2)}) %all-to-all-start.1) | async-done | bytes 524320 | tf_op jit(solution)/shard_map/all_to_all | solution.py:248
  58.7 4.3 %collective-permute-done.1.v_oth = bf16[2048,128]{1,0:T(8,128)(2,1)} collective-permute-done((bf16[2048,128]{1,0:T(8,128)(2,1)S(1)}, bf16[2048,128]{1,0:T(8,128)(2,1)}, u32[]{:S(2)}, u32[]{:S(2)}) %collective-permute-start.1) | collective-permute-done | bytes 524320 | tf_op jit(solution)/shard_map/ppermute | solution.py:152
  63.0 16.5 %attention.1 = (bf16[128,2048]{1,0:T(8,128)(2,1)}, f32[128,2048]{1,0:T(8,128)}, bf16[128,2048]{1,0:T(8,128)(2,1)}) custom-call(s32[6]{0:T(128)} %starts.1, s32[1]{0:T(128)} %bitcast.2.where_ref, bf16[2048,128]{1,0:T(8,128)(2,1)} %bitcast.39, bf16[2048,128]{1,0:T(8,128)(2,1)} %bitcast.40, bf16[2048,128]{1,0:T(8,128)(2,1)} %bitcast.36, ...), custom_call_target="tpu_custom_call" | custom-call | tf_op jit(solution)/shard_map/attention/pallas_call | solution.py:128
  79.5 8.5 %collective-permute-start.2 = (bf16[128,2048]{1,0:T(8,128)(2,1)}, bf16[128,2048]{1,0:T(8,128)(2,1)S(1)}, u32[]{:S(2)}, u32[]{:S(2)}) collective-permute-start(bf16[128,2048]{1,0:T(8,128)(2,1)} %get-tuple-element.21), channel_id=1, source_target_pairs={{0,8},{8,0},{1,9},{9,1},{2,10},{10,2},{3,11},{11,3},{4,12},{12,4},... | collective-permute-start | bytes 1572872 | tf_op jit(solution)/shard_map/ppermute | solution.py:152
  93.0 3.6 %collective-permute-done.2 = bf16[128,2048]{1,0:T(8,128)(2,1)S(1)} collective-permute-done((bf16[128,2048]{1,0:T(8,128)(2,1)}, bf16[128,2048]{1,0:T(8,128)(2,1)S(1)}, u32[]{:S(2)}, u32[]{:S(2)}) %collective-permute-start.2) | collective-permute-done | bytes 524320 | tf_op jit(solution)/shard_map/ppermute | solution.py:152
  99.3 3.8 %collective-permute-start.6 = (bf16[64,2048]{1,0:T(8,128)(2,1)S(1)}, bf16[64,2048]{1,0:T(8,128)(2,1)S(1)}, u32[]{:S(2)}, u32[]{:S(2)}) collective-permute-start(bf16[64,2048]{1,0:T(8,128)(2,1)S(1)} %slice.24), channel_id=1, source_target_pairs={{0,2},{2,4},{4,6},{6,0},{1,3},{3,5},{5,7},{7,1},{8,10},{10,12},{12... | collective-permute-start | bytes 786440 | tf_op jit(solution)/shard_map/ppermute | solution.py:152
  103.1 5.3 %collective-permute-start.8 = (bf16[128,2048]{1,0:T(8,128)(2,1)S(1)}, bf16[128,2048]{1,0:T(8,128)(2,1)}, u32[]{:S(2)}, u32[]{:S(2)}) collective-permute-start(bf16[128,2048]{1,0:T(8,128)(2,1)S(1)} %collective-permute-done.5), channel_id=1, source_target_pairs={{0,0},{34,32},{68,64},{102,96},{8,16},{42,48},{76,80},{110,112},{1... | collective-permute-start | bytes 1572872 | tf_op jit(solution)/shard_map/ppermute | solution.py:284
  114.6 3.2 %collective-permute-start.7 = (bf16[64,2048]{1,0:T(8,128)(2,1)S(1)}, bf16[64,2048]{1,0:T(8,128)(2,1)}, u32[]{:S(2)}, u32[]{:S(2)}) collective-permute-start(bf16[64,2048]{1,0:T(8,128)(2,1)S(1)} %slice.25), channel_id=1, source_target_pairs={{0,6},{2,0},{4,2},{6,4},{1,7},{3,1},{5,3},{7,5},{8,14},{10,8},{12,... | collective-permute-start | bytes 786440 | tf_op jit(solution)/shard_map/ppermute | solution.py:152
  117.8 4.9 %collective-permute-done.7.refs_4_ = bf16[64,2048]{1,0:T(8,128)(2,1)} collective-permute-done((bf16[64,2048]{1,0:T(8,128)(2,1)S(1)}, bf16[64,2048]{1,0:T(8,128)(2,1)}, u32[]{:S(2)}, u32[]{:S(2)}) %collective-permute-start.7) | collective-permute-done | bytes 262176 | tf_op jit(solution)/shard_map/ppermute | solution.py:152
  122.7 7.3 %collective-permute-done.9.refs_1_ = bf16[128,2048]{1,0:T(8,128)(2,1)S(1)} collective-permute-done((bf16[128,2048]{1,0:T(8,128)(2,1)S(1)}, bf16[128,2048]{1,0:T(8,128)(2,1)S(1)}, u32[]{:S(2)}, u32[]{:S(2)}) %collective-permute-start.9) | collective-permute-done | bytes 524320 | tf_op jit(solution)/shard_map/ppermute | solution.py:152
  133.1 15.9 %collective-permute-done.22 = bf16[128,2048]{1,0:T(8,128)(2,1)} collective-permute-done((bf16[128,2048]{1,0:T(8,128)(2,1)}, bf16[128,2048]{1,0:T(8,128)(2,1)}, u32[]{:S(2)}, u32[]{:S(2)}) %collective-permute-start.22) | collective-permute-done | bytes 524320 | tf_op jit(solution)/shard_map/ppermute | solution.py:290
  164.3 3.2 %collective-permute-start.19 = (bf16[512,2048]{1,0:T(8,128)(2,1)}, bf16[512,2048]{1,0:T(8,128)(2,1)S(1)}, u32[]{:S(2)}, u32[]{:S(2)}) collective-permute-start(bf16[512,2048]{1,0:T(8,128)(2,1)} %stack.15.refs_1_), channel_id=1, source_target_pairs={{0,6},{2,0},{4,2},{6,4},{1,7},{3,1},{5,3},{7,5},{8,14},{10,8},{12,... | collective-permute-start | bytes 6291464 | tf_op jit(solution)/shard_map/ppermute | solution.py:152
  167.6 38.2 %collective-permute-done.12.refs_2_ = bf16[512,2048]{1,0:T(8,128)(2,1)S(1)} collective-permute-done((bf16[512,2048]{1,0:T(8,128)(2,1)}, bf16[512,2048]{1,0:T(8,128)(2,1)S(1)}, u32[]{:S(2)}, u32[]{:S(2)}) %collective-permute-start.12) | collective-permute-done | bytes 2097184 | tf_op jit(solution)/shard_map/ppermute | solution.py:152
  209.3 3.2 %collective-permute-start.15 = (bf16[256,2048]{1,0:T(8,128)(2,1)}, bf16[256,2048]{1,0:T(8,128)(2,1)}, u32[]{:S(2)}, u32[]{:S(2)}) collective-permute-start(bf16[256,2048]{1,0:T(8,128)(2,1)} %slice.33), channel_id=1, source_target_pairs={{0,9},{1,0},{8,1},{9,8},{2,11},{3,2},{10,3},{11,10},{4,13},{5,4},{... | collective-permute-start | bytes 3145736 | tf_op jit(solution)/shard_map/ppermute | solution.py:152
  219.1 13.7 %collective-permute-done.14.refs_4_ = bf16[256,2048]{1,0:T(8,128)(2,1)} collective-permute-done((bf16[256,2048]{1,0:T(8,128)(2,1)}, bf16[256,2048]{1,0:T(8,128)(2,1)}, u32[]{:S(2)}, u32[]{:S(2)}) %collective-permute-start.14) | collective-permute-done | bytes 1048608 | tf_op jit(solution)/shard_map/ppermute | solution.py:152
  234.3 11.3 %input_factor.1 = f32[1024,512]{1,0:T(8,128)} custom-call(s32[2]{0:T(128)} %pad_add_fusion.refs_0_, bf16[512,2048]{1,0:T(8,128)(2,1)} %stack.14.refs_1_, bf16[512,2048]{1,0:T(8,128)(2,1)} %copy-done.1, bf16[512,2048]{1,0:T(8,128)(2,1)} %collective-permute-done.13.refs_3_, bf16[256,2048]{1,0:T(8,128)(2,1)} %collective-permute-done.14.refs_4_, ...), custom_call_target="tpu_custom_call" | custom-call | tf_op jit(solution)/shard_map/input_factor/pallas_call | solution.py:232
  246.7 11.3 %grad_factor.1 = f32[1024,512]{1,0:T(8,128)} custom-call(s32[2]{0:T(128)} %pad_add_fusion.refs_0_, bf16[512,2048]{1,0:T(8,128)(2,1)} %stack.15.refs_1_, bf16[512,2048]{1,0:T(8,128)(2,1)} %copy-done.2, bf16[512,2048]{1,0:T(8,128)(2,1)} %copy-done.3, bf16[256,2048]{1,0:T(8,128)(2,1)} %collective-permute-done.20.refs_4_, bf16[256,2048]{1,0:T(8,128)(2,1)} %copy-done.13, ...), custom_call_target="tpu_custom_call" | custom-call | tf_op jit(solution)/shard_map/grad_factor/pallas_call | solution.py:232
  (93 shorter events, 53.0 us)
Async XLA Ops:
  9.1 14.8 %all-to-all-start.2 = ((bf16[512,4,128]{2,0,1:T(8,128)(2,1)}), bf16[512,4,128]{2,0,1:T(8,128)(2,1)S(1)}, u32[]{:S(2)}, u32[]{:S(2)}) async-start(bf16[512,4,128]{2,0,1:T(8,128)(2,1)} %copy_bitcast_fusion.1), calls=%async_computation.2 | async-start | bytes 1048576 | tf_op jit(solution)/shard_map/all_to_all | solution.py:248
  23.9 11.7 %all-to-all-start.3 = ((bf16[512,4,128]{2,0,1:T(8,128)(2,1)}), bf16[512,4,128]{2,0,1:T(8,128)(2,1)S(1)}, u32[]{:S(2)}, u32[]{:S(2)}) async-start(bf16[512,4,128]{2,0,1:T(8,128)(2,1)} %copy_bitcast_fusion), calls=%async_computation.3 | async-start | bytes 1048576 | tf_op jit(solution)/shard_map/all_to_all | solution.py:248
  35.6 11.5 %all-to-all-start = ((bf16[512,4,128]{2,0,1:T(8,128)(2,1)}), bf16[512,4,128]{2,0,1:T(8,128)(2,1)S(1)}, u32[]{:S(2)}, u32[]{:S(2)}) async-start(bf16[512,4,128]{2,0,1:T(8,128)(2,1)} %copy_bitcast_fusion.3), calls=%async_computation | async-start | bytes 1048576 | tf_op jit(solution)/shard_map/all_to_all | solution.py:248
  39.1 19.6 %collective-permute-start = (bf16[2048,128]{1,0:T(8,128)(2,1)S(1)}, bf16[2048,128]{1,0:T(8,128)(2,1)S(1)}, u32[]{:S(2)}, u32[]{:S(2)}) collective-permute-start(bf16[2048,128]{1,0:T(8,128)(2,1)S(1)} %bitcast.35), channel_id=1, source_target_pairs={{0,8},{8,0},{1,9},{9,1},{2,10},{10,2},{3,11},{11,3},{4,12},{12,4},... | collective-permute-start | bytes 1572872 | tf_op jit(solution)/shard_map/ppermute | solution.py:152
  42.2 20.8 %collective-permute-start.1 = (bf16[2048,128]{1,0:T(8,128)(2,1)S(1)}, bf16[2048,128]{1,0:T(8,128)(2,1)}, u32[]{:S(2)}, u32[]{:S(2)}) collective-permute-start(bf16[2048,128]{1,0:T(8,128)(2,1)S(1)} %bitcast.37), channel_id=1, source_target_pairs={{0,8},{8,0},{1,9},{9,1},{2,10},{10,2},{3,11},{11,3},{4,12},{12,4},... | collective-permute-start | bytes 1572872 | tf_op jit(solution)/shard_map/ppermute | solution.py:152
  47.1 11.5 %all-to-all-start.1 = ((bf16[512,4,128]{2,0,1:T(8,128)(2,1)}), bf16[512,4,128]{2,0,1:T(8,128)(2,1)S(1)}, u32[]{:S(2)}, u32[]{:S(2)}) async-start(bf16[512,4,128]{2,0,1:T(8,128)(2,1)} %copy_bitcast_fusion.2), calls=%async_computation.1 | async-start | bytes 1048576 | tf_op jit(solution)/shard_map/all_to_all | solution.py:248
  50.6 183.7 %all-gather.3.cloned.1.call-start = ((), (), s32[]{:S(2)}) async-start(), calls=%async_computation.4 | async-start | bytes 4718592 | tf_op jit(solution)/shard_map/all_gather | solution.py:292
  79.5 17.0 %collective-permute-start.2 = (bf16[128,2048]{1,0:T(8,128)(2,1)}, bf16[128,2048]{1,0:T(8,128)(2,1)S(1)}, u32[]{:S(2)}, u32[]{:S(2)}) collective-permute-start(bf16[128,2048]{1,0:T(8,128)(2,1)} %get-tuple-element.21), channel_id=1, source_target_pairs={{0,8},{8,0},{1,9},{9,1},{2,10},{10,2},{3,11},{11,3},{4,12},{12,4},... | collective-permute-start | bytes 1572872 | tf_op jit(solution)/shard_map/ppermute | solution.py:152
  88.0 11.2 %collective-permute-start.3 = (bf16[128,2048]{1,0:T(8,128)(2,1)}, bf16[128,2048]{1,0:T(8,128)(2,1)S(1)}, u32[]{:S(2)}, u32[]{:S(2)}) collective-permute-start(bf16[128,2048]{1,0:T(8,128)(2,1)} %get-tuple-element.23.refs_0_), channel_id=1, source_target_pairs={{0,2},{2,4},{4,6},{6,0},{1,3},{3,5},{5,7},{7,1},{8,10},{10,12},{12... | collective-permute-start | bytes 1572872 | tf_op jit(solution)/shard_map/ppermute | solution.py:152
  99.3 15.3 %collective-permute-start.6 = (bf16[64,2048]{1,0:T(8,128)(2,1)S(1)}, bf16[64,2048]{1,0:T(8,128)(2,1)S(1)}, u32[]{:S(2)}, u32[]{:S(2)}) collective-permute-start(bf16[64,2048]{1,0:T(8,128)(2,1)S(1)} %slice.24), channel_id=1, source_target_pairs={{0,2},{2,4},{4,6},{6,0},{1,3},{3,5},{5,7},{7,1},{8,10},{10,12},{12... | collective-permute-start | bytes 786440 | tf_op jit(solution)/shard_map/ppermute | solution.py:152
  103.1 19.6 %collective-permute-start.8 = (bf16[128,2048]{1,0:T(8,128)(2,1)S(1)}, bf16[128,2048]{1,0:T(8,128)(2,1)}, u32[]{:S(2)}, u32[]{:S(2)}) collective-permute-start(bf16[128,2048]{1,0:T(8,128)(2,1)S(1)} %collective-permute-done.5), channel_id=1, source_target_pairs={{0,0},{34,32},{68,64},{102,96},{8,16},{42,48},{76,80},{110,112},{1... | collective-permute-start | bytes 1572872 | tf_op jit(solution)/shard_map/ppermute | solution.py:284
  109.8 20.2 %collective-permute-start.9 = (bf16[128,2048]{1,0:T(8,128)(2,1)S(1)}, bf16[128,2048]{1,0:T(8,128)(2,1)S(1)}, u32[]{:S(2)}, u32[]{:S(2)}) collective-permute-start(bf16[128,2048]{1,0:T(8,128)(2,1)S(1)} %add_convert_fusion.refs_0_), channel_id=1, source_target_pairs={{0,1},{1,8},{8,9},{9,0},{2,3},{3,10},{10,11},{11,2},{4,5},{5,12},{... | collective-permute-start | bytes 1572872 | tf_op jit(solution)/shard_map/ppermute | solution.py:152
  110.5 20.6 %collective-permute-start.10 = (bf16[128,2048]{1,0:T(8,128)(2,1)S(1)}, bf16[128,2048]{1,0:T(8,128)(2,1)S(1)}, u32[]{:S(2)}, u32[]{:S(2)}) collective-permute-start(bf16[128,2048]{1,0:T(8,128)(2,1)S(1)} %add_convert_fusion.refs_0_), channel_id=1, source_target_pairs={{0,9},{1,0},{8,1},{9,8},{2,11},{3,2},{10,3},{11,10},{4,13},{5,4},{... | collective-permute-start | bytes 1572872 | tf_op jit(solution)/shard_map/ppermute | solution.py:152
  113.1 18.1 %collective-permute-start.11 = (bf16[128,2048]{1,0:T(8,128)(2,1)S(1)}, bf16[128,2048]{1,0:T(8,128)(2,1)}, u32[]{:S(2)}, u32[]{:S(2)}) collective-permute-start(bf16[128,2048]{1,0:T(8,128)(2,1)S(1)} %add_convert_fusion.refs_0_), channel_id=1, source_target_pairs={{0,0},{2,34},{4,68},{6,102},{8,8},{10,42},{12,76},{14,110},{16,16}... | collective-permute-start | bytes 1572872 | tf_op jit(solution)/shard_map/ppermute | solution.py:282
  131.2 114.6 %all-gather.5.cloned.1.call-start = ((), (), s32[]{:S(2)}) async-start(), calls=%async_computation.5 | async-start | bytes 4718592 | tf_op jit(solution)/shard_map/all_gather | solution.py:293
  131.2 17.8 %collective-permute-start.22 = (bf16[128,2048]{1,0:T(8,128)(2,1)}, bf16[128,2048]{1,0:T(8,128)(2,1)}, u32[]{:S(2)}, u32[]{:S(2)}) collective-permute-start(bf16[128,2048]{1,0:T(8,128)(2,1)} %collective-permute-done.11), channel_id=1, source_target_pairs={{0,0},{34,32},{68,64},{102,96},{8,16},{42,48},{76,80},{110,112},{1... | collective-permute-start | bytes 1572872 | tf_op jit(solution)/shard_map/ppermute | solution.py:290
  156.8 49.0 %collective-permute-start.12 = (bf16[512,2048]{1,0:T(8,128)(2,1)}, bf16[512,2048]{1,0:T(8,128)(2,1)S(1)}, u32[]{:S(2)}, u32[]{:S(2)}) collective-permute-start(bf16[512,2048]{1,0:T(8,128)(2,1)} %stack.14.refs_1_), channel_id=1, source_target_pairs={{0,1},{1,8},{8,9},{9,0},{2,3},{3,10},{10,11},{11,2},{4,5},{5,12},{... | collective-permute-start | bytes 6291464 | tf_op jit(solution)/shard_map/ppermute | solution.py:152
  157.0 49.9 %collective-permute-start.13 = (bf16[512,2048]{1,0:T(8,128)(2,1)}, bf16[512,2048]{1,0:T(8,128)(2,1)}, u32[]{:S(2)}, u32[]{:S(2)}) collective-permute-start(bf16[512,2048]{1,0:T(8,128)(2,1)} %stack.14.refs_1_), channel_id=1, source_target_pairs={{0,9},{1,0},{8,1},{9,8},{2,11},{3,2},{10,3},{11,10},{4,13},{5,4},{... | collective-permute-start | bytes 6291464 | tf_op jit(solution)/shard_map/ppermute | solution.py:152
  164.3 48.1 %collective-permute-start.18 = (bf16[512,2048]{1,0:T(8,128)(2,1)}, bf16[512,2048]{1,0:T(8,128)(2,1)S(1)}, u32[]{:S(2)}, u32[]{:S(2)}) collective-permute-start(bf16[512,2048]{1,0:T(8,128)(2,1)} %stack.15.refs_1_), channel_id=1, source_target_pairs={{0,2},{2,4},{4,6},{6,0},{1,3},{3,5},{5,7},{7,1},{8,10},{10,12},{12... | collective-permute-start | bytes 6291464 | tf_op jit(solution)/shard_map/ppermute | solution.py:152
  164.3 50.1 %collective-permute-start.19 = (bf16[512,2048]{1,0:T(8,128)(2,1)}, bf16[512,2048]{1,0:T(8,128)(2,1)S(1)}, u32[]{:S(2)}, u32[]{:S(2)}) collective-permute-start(bf16[512,2048]{1,0:T(8,128)(2,1)} %stack.15.refs_1_), channel_id=1, source_target_pairs={{0,6},{2,0},{4,2},{6,4},{1,7},{3,1},{5,3},{7,5},{8,14},{10,8},{12,... | collective-permute-start | bytes 6291464 | tf_op jit(solution)/shard_map/ppermute | solution.py:152
  206.9 25.8 %collective-permute-start.14 = (bf16[256,2048]{1,0:T(8,128)(2,1)}, bf16[256,2048]{1,0:T(8,128)(2,1)}, u32[]{:S(2)}, u32[]{:S(2)}) collective-permute-start(bf16[256,2048]{1,0:T(8,128)(2,1)} %slice.32), channel_id=1, source_target_pairs={{0,1},{1,8},{8,9},{9,0},{2,3},{3,10},{10,11},{11,2},{4,5},{5,12},{... | collective-permute-start | bytes 3145736 | tf_op jit(solution)/shard_map/ppermute | solution.py:152
  209.3 25.1 %collective-permute-start.15 = (bf16[256,2048]{1,0:T(8,128)(2,1)}, bf16[256,2048]{1,0:T(8,128)(2,1)}, u32[]{:S(2)}, u32[]{:S(2)}) collective-permute-start(bf16[256,2048]{1,0:T(8,128)(2,1)} %slice.33), channel_id=1, source_target_pairs={{0,9},{1,0},{8,1},{9,8},{2,11},{3,2},{10,3},{11,10},{4,13},{5,4},{... | collective-permute-start | bytes 3145736 | tf_op jit(solution)/shard_map/ppermute | solution.py:152
  213.6 32.0 %collective-permute-start.20 = (bf16[256,2048]{1,0:T(8,128)(2,1)}, bf16[256,2048]{1,0:T(8,128)(2,1)}, u32[]{:S(2)}, u32[]{:S(2)}) collective-permute-start(bf16[256,2048]{1,0:T(8,128)(2,1)} %slice.34), channel_id=1, source_target_pairs={{0,2},{2,4},{4,6},{6,0},{1,3},{3,5},{5,7},{7,1},{8,10},{10,12},{12... | collective-permute-start | bytes 3145736 | tf_op jit(solution)/shard_map/ppermute | solution.py:152
  215.8 29.8 %collective-permute-start.21 = (bf16[256,2048]{1,0:T(8,128)(2,1)S(1)}, bf16[256,2048]{1,0:T(8,128)(2,1)S(1)}, u32[]{:S(2)}, u32[]{:S(2)}) collective-permute-start(bf16[256,2048]{1,0:T(8,128)(2,1)S(1)} %slice.35), channel_id=1, source_target_pairs={{0,6},{2,0},{4,2},{6,4},{1,7},{3,1},{5,3},{7,5},{8,14},{10,8},{12,... | collective-permute-start | bytes 3145736 | tf_op jit(solution)/shard_map/ppermute | solution.py:152
  (24 other events, 419.3 us)
Sparse Core Ops, SparseCore 0:
  131.3 29.0 all-gather.2
  162.1 32.0 all-gather.4

commit v3 on v2

--- a/solution.py
+++ b/solution.py
@@ -11,27 +11,34 @@
 
 HEAD_DIM = 128
 X = ("xh", "xl")
+RING = (0, 3, 1, 2)
 MASK_FLOOR = -1e30
 KEY_STEP = 512
 QUERY_STEP = 512
 VMEM_BYTES = 56 * 1024 * 1024
 
 
-def attention_kernel(
-    starts, where_ref, q_ref, g_ref, k_own, k_oth, v_own, v_oth,
-    att_ref, near_ref, far_ref,
-    k_all, v_all, v_turned, scores, grads, sems,
-):
+def attention_kernel(starts, where_ref, *refs):
+    kv_own, kv_oth, qg = refs[:4], refs[4:8], refs[8:12]
+    att_ref, near_ref, far_ref = refs[12:15]
+    k_all, v_all, q_ref, g_ref, v_turned, scores, grads, sems = refs[15:]
     half = q_ref.shape[0]
-    half_id = where_ref[0]
+    part = half // 4
+    half_id, z = where_ref[0], where_ref[1]
     own_at = pl.multiple_of(half_id * half, half)
     oth_at = pl.multiple_of((1 - half_id) * half, half)
-    copies = [
-        pltpu.make_async_copy(k_own, k_all.at[pl.ds(own_at, half)], sems.at[0]),
-        pltpu.make_async_copy(k_oth, k_all.at[pl.ds(oth_at, half)], sems.at[1]),
-        pltpu.make_async_copy(v_own, v_all.at[pl.ds(own_at, half)], sems.at[2]),
-        pltpu.make_async_copy(v_oth, v_all.at[pl.ds(oth_at, half)], sems.at[3]),
-    ]
+    copies = []
+    for pieces, base, targets in (
+        (kv_own, own_at, (k_all, v_all)), (kv_oth, oth_at, (k_all, v_all)), (qg, 0, (q_ref, g_ref))
+    ):
+        for step, piece in zip(RING, pieces):
+            at = pl.multiple_of(base + ((z + step) % 4) * part, part)
+            for n, target in enumerate(targets):
+                copies.append(
+                    pltpu.make_async_copy(
+                        piece.at[pl.ds(n * part, part)], target.at[pl.ds(at, part)], sems.at[len(copies)]
+                    )
+                )
     for copy in copies:
         copy.start()
     grads[...] = jnp.zeros_like(grads)
@@ -120,8 +127,8 @@
         far_ref[:, at : at + KEY_STEP] = grads[pl.ds(oth_at + at, KEY_STEP), :].T.astype(jnp.bfloat16)
 
 
-def attention(starts, half_id, q, g, k_own, k_oth, v_own, v_oth):
-    half = q.shape[0]
+def attention(starts, where, kv_own, kv_oth, qg):
+    half = 2 * qg[0].shape[0]
     hbm = pl.BlockSpec(memory_space=pl.ANY)
     vmem = pl.BlockSpec(memory_space=pltpu.VMEM)
     smem = pl.BlockSpec(memory_space=pltpu.SMEM)
@@ -132,19 +139,21 @@
             jax.ShapeDtypeStruct((HEAD_DIM, half), jnp.float32),
             jax.ShapeDtypeStruct((HEAD_DIM, half), jnp.bfloat16),
         ),
-        in_specs=[smem, smem, vmem, vmem, hbm, hbm, hbm, hbm],
+        in_specs=[smem, smem] + [hbm] * 12,
         out_specs=(vmem, vmem, vmem),
         scratch_shapes=[
             pltpu.VMEM((2 * half, HEAD_DIM), jnp.bfloat16),
             pltpu.VMEM((2 * half, HEAD_DIM), jnp.bfloat16),
+            pltpu.VMEM((half, HEAD_DIM), jnp.bfloat16),
+            pltpu.VMEM((half, HEAD_DIM), jnp.bfloat16),
             pltpu.VMEM((HEAD_DIM, 2 * half), jnp.bfloat16),
             pltpu.VMEM((2 * half, QUERY_STEP), jnp.float32),
             pltpu.VMEM((2 * half, HEAD_DIM), jnp.float32),
-            pltpu.SemaphoreType.DMA((4,)),
+            pltpu.SemaphoreType.DMA((24,)),
         ],
         compiler_params=pltpu.CompilerParams(vmem_limit_bytes=VMEM_BYTES),
         name="attention",
-    )(starts, half_id, q, g, k_own, k_oth, v_own, v_oth)
+    )(starts, where, *kv_own, *kv_oth, *qg)
 
 
 def shifted(x, axis, by):
@@ -161,9 +170,42 @@
     return shifted(below[:half], axis, 1), shifted(above[half:], axis, -1)
 
 
-def ring(x, axis):
-    below, above = near_ring(x, axis)
-    return (x, below, above, *far_ring(below, above, axis))
+def heads_kernel(z_ref, *refs):
+    sources, outs, sems = refs[:2], refs[2:6], refs[6]
+    rows = sources[0].shape[0]
+    copies = []
+    for k, out in enumerate(outs):
+        head = (z_ref[0] + k) % 4
+        for n, source in enumerate(sources):
+            copies.append(
+                pltpu.make_async_copy(
+                    source.at[:, pl.ds(pl.multiple_of(head * HEAD_DIM, HEAD_DIM), HEAD_DIM)],
+                    out.at[pl.ds(n * rows, rows)], sems.at[len(copies)],
+                )
+            )
+    for copy in copies:
+        copy.start()
+    for copy in copies:
+        copy.wait()
+
+
+def by_head(z, first, second):
+    rows = first.shape[0]
+    shape = jax.ShapeDtypeStruct((2 * rows, HEAD_DIM), first.dtype)
+    hbm = pl.BlockSpec(memory_space=pl.ANY)
+    vmem = pl.BlockSpec(memory_space=pltpu.VMEM)
+    return pl.pallas_call(
+        heads_kernel,
+        out_shape=(shape,) * 4,
+        in_specs=[pl.BlockSpec(memory_space=pltpu.SMEM), hbm, hbm],
+        out_specs=(vmem,) * 4,
+        scratch_shapes=[pltpu.SemaphoreType.DMA((8,))],
+        name="by_head",
+    )(z, first, second)
+
+
+def swap_heads(parts):
+    return parts[0], shifted(parts[1], "z", 1), shifted(parts[3], "z", -1), shifted(parts[2], "z", 2)
 
 
 def stack_kernel(*refs):
@@ -185,9 +227,10 @@
     )(*parts)
 
 
-def factor_kernel(place, *refs, which, count):
-    z_first = which == 0
-    row_refs, (col_ref, out, rows, cols, sems) = refs[:5], refs[5:]
+def factor_kernel(place, *refs, count, plan, blocks, aliased):
+    n_pieces = len(refs) - 6 - aliased
+    pieces, col_ref = refs[:n_pieces], refs[n_pieces]
+    out, rows, cols, result, sems = refs[n_pieces + 1 + aliased :]
     x, z = place[0], place[1]
     block = HEAD_DIM
     copies = []
@@ -197,55 +240,86 @@
         copy.start()
         copies.append(copy)
 
-    ring_steps = (0, 3, 1, 2)
     line = 4 - (x // 2) * 2 - z // 2
     for n in range(8):
         at = ((n // 2 + line) % 4) * block
         start(col_ref.at[pl.ds(n * block, block)], cols.at[n % 2, pl.ds(pl.multiple_of(at, block), block)])
-    for k in range(5):
-        outer = ring_steps[min(k, 3)]
-        inners = ((0, 1, 2, 3), (0, 1, 2, 3), (0, 1, 2, 3), (0, 1), (2, 3))[k]
-        for n, slot in enumerate(inners):
-            inner = ring_steps[slot]
-            zz = (z + (inner if z_first else outer)) % 4
-            xx = (x + (outer if z_first else inner)) % 4
-            at = pl.multiple_of(((xx % 2) * 4 + zz) * block, block)
-            start(row_refs[k].at[pl.ds(n * block, block)], rows.at[xx // 2, pl.ds(at, block)])
+    targets, out_rows = plan(x, z)
+    for piece, pair in zip(pieces, targets):
+        for n, (which, local) in enumerate(pair):
+            at = pl.multiple_of(local * block, block)
+            start(piece.at[pl.ds(n * block, block)], rows.at[which, pl.ds(at, block)])
     for copy in copies:
         copy.wait()
-    step = 256
-    for at in range(0, rows.shape[1], step):
-        total = None
-        for who in range(2):
-            part = lax.dot_general(
-                rows[who, at : at + step, :], cols[who], (((1,), (1,)), ((), ())),
-                preferred_element_type=jnp.float32,
-            )
-            total = part if total is None else total + part
-        out[at : at + step, :] = total * (1.0 / count)
-
-
-def factor(place, rows, cols, which, count):
+    total = None
+    for which in range(2):
+        part = lax.dot_general(
+            rows[which], cols[which], (((1,), (1,)), ((), ())), preferred_element_type=jnp.float32
+        )
+        total = part if total is None else total + part
+    result[...] = total * (1.0 / count)
+    stores = []
+    for local in range(blocks):
+        row = pl.multiple_of(out_rows[local] * block, block)
+        store = pltpu.make_async_copy(
+            result.at[pl.ds(local * block, block)], out.at[pl.ds(row, block)], sems.at[24 + local]
+        )
+        store.start()
+        stores.append(store)
+    for store in stores:
+        store.wait()
+
+
+def along_x_pieces(pieces):
+    def plan(x, z):
+        targets = [[((x + RING[outer]) % 4 // 2, slot) for slot in slots] for outer, slots in pieces]
+        cols_at = (x + RING[pieces[0][0]]) % 2
+        return targets, [cols_at * 4 + (z + RING[slot]) % 4 for slot in range(4)]
+
+    return plan, 4
+
+
+def along_z_pieces(pieces):
+    groups = list(dict.fromkeys(outer for outer, _ in pieces))
+
+    def plan(x, z):
+        targets = []
+        for outer, slots in pieces:
+            at = [(x + RING[slot]) % 4 for slot in slots]
+            targets.append([(xx // 2, groups.index(outer) * 2 + xx % 2) for xx in at])
+        return targets, [c * 4 + (z + RING[g]) % 4 for g in groups for c in range(2)]
+
+    return plan, 2 * len(groups)
+
+
+def factor_part(place, groups, outers, cols, layout, count, name, into=None):
+    held = []
+    for outer in outers:
+        held += [(3, (0, 1), groups[3]), (3, (2, 3), groups[4])] if outer == 3 else [(outer, (0, 1, 2, 3), groups[outer])]
+    pieces = [piece for _, _, piece in held]
+    plan, blocks = layout([(outer, slots) for outer, slots, _ in held])
     tokens = cols.shape[1]
     hbm = pl.BlockSpec(memory_space=pl.ANY)
-    kernel = lambda *refs: factor_kernel(*refs, which=which, count=count)
+    aliased = into is not None
+    kernel = functools.partial(
+        factor_kernel, count=count, plan=plan, blocks=blocks, aliased=int(aliased)
+    )
+    args = [place, *pieces, cols] + ([into] if aliased else [])
     return pl.pallas_call(
         kernel,
         out_shape=jax.ShapeDtypeStruct((8 * HEAD_DIM, 4 * HEAD_DIM), jnp.float32),
-        in_specs=[pl.BlockSpec(memory_space=pltpu.SMEM)] + [hbm] * 6,
-        out_specs=pl.BlockSpec(memory_space=pltpu.VMEM),
+        in_specs=[pl.BlockSpec(memory_space=pltpu.SMEM)] + [hbm] * (len(args) - 1),
+        out_specs=hbm,
+        input_output_aliases={len(args) - 1: 0} if aliased else {},
         scratch_shapes=[
-            pltpu.VMEM((2, 8 * HEAD_DIM, tokens), jnp.bfloat16),
+            pltpu.VMEM((2, blocks * HEAD_DIM, tokens), jnp.bfloat16),
             pltpu.VMEM((2, 4 * HEAD_DIM, tokens), jnp.bfloat16),
-            pltpu.SemaphoreType.DMA((24,)),
+            pltpu.VMEM((blocks * HEAD_DIM, 4 * HEAD_DIM), jnp.float32),
+            pltpu.SemaphoreType.DMA((32,)),
         ],
         compiler_params=pltpu.CompilerParams(vmem_limit_bytes=VMEM_BYTES),
-        name="grad_factor" if which else "input_factor",
-    )(place, *rows, cols)
-
-
-def by_head(x):
-    return lax.all_to_all(x, "z", split_axis=1, concat_axis=0, tiled=True)
+        name=name,
+    )(*args)
 
 
 def column_moves():
@@ -263,14 +337,12 @@
     all_tokens = query_in.shape[0] * 8
     xh, z = lax.axis_index("xh"), lax.axis_index("z")
     place = jnp.stack([lax.axis_index(X), z]).astype(jnp.int32)
-    k_own = by_head(key_in)
-    k_oth = shifted(k_own, "xh", 1)
-    v_own = by_head(value_in)
-    v_oth = shifted(v_own, "xh", 1)
-    q, g = by_head(query_in), by_head(out_grads)
-    attended, near, far = attention(
-        doc_starts, xh.astype(jnp.int32)[None], q, g, k_own, k_oth, v_own, v_oth
-    )
+    z_only = z.astype(jnp.int32)[None]
+    kv_own = swap_heads(by_head(z_only, key_in, value_in))
+    kv_oth = tuple(shifted(piece, "xh", 1) for piece in kv_own)
+    qg = swap_heads(by_head(z_only, query_in, out_grads))
+    where = jnp.stack([xh, z]).astype(jnp.int32)
+    attended, near, far = attention(doc_starts, where, kv_own, kv_oth, qg)
     line = ("y", "core", "xh", "z")
     along_y, in_plane = column_moves()
     far = shifted(far, "xh", 1)
@@ -286,15 +358,27 @@
         (a_near, a_far, a_col, value_grads, g_near, g_col)
     )
     group_a = stacked((attended, *a_near, *a_far))
+    group_a, g_near, g_col = lax.optimization_barrier((group_a, g_near, g_col))
+    a_near = near_ring(group_a, X)
     g_far = far_ring(*g_near, X)
     g_col = lax.ppermute(g_col, line, in_plane)
+    cols_a = lax.all_gather(a_col, ("y", "core"), axis=0, tiled=True)
     group_g = stacked((value_grads, *g_near, *g_far))
-    cols_a = lax.all_gather(a_col, ("y", "core"), axis=0, tiled=True)
+    g_near = near_ring(group_g, "z")
+    g_col, _ = lax.optimization_barrier((g_col, group_g))
     cols_g = lax.all_gather(g_col, ("y", "core"), axis=0, tiled=True)
-    rows_a = ring(group_a, X)
-    rows_g = ring(group_g, "z")
-    input_factor = factor(place, rows_a, cols_a, 0, all_tokens)
-    grad_factor = factor(place, rows_g, cols_g, 1, all_tokens)
+    a_far = far_ring(*a_near, X)
+    g_far = far_ring(*g_near, "z")
+    rows_a, rows_g = (group_a, *a_near, *a_far), (group_g, *g_near, *g_far)
+    input_factor = factor_part(place, rows_a, (1, 2), cols_a, along_x_pieces, all_tokens, "input_near")
+    grad_factor = factor_part(place, rows_g, (0, 1, 2), cols_g, along_z_pieces, all_tokens, "grad_near")
+    input_factor, grad_factor = lax.optimization_barrier((input_factor, grad_factor))
+    input_factor = factor_part(
+        place, rows_a, (0, 3), cols_a, along_x_pieces, all_tokens, "input_far", input_factor
+    )
+    grad_factor = factor_part(
+        place, rows_g, (3,), cols_g, along_z_pieces, all_tokens, "grad_far", grad_factor
+    )
     return (input_factor, grad_factor)
 
 

time: 269 us -> 252 us (0.937)
  Pallas kernels: 45.2 us -> 63.4 us
  waiting for transfers between devices: 122 us -> 105 us
  starting transfers between devices: 68.4 us -> 53.4 us
    all_to_all x4 -> x0, waiting for transfers between devices: 27.5 us -> none  [by_head(): return lax.all_to_all(x, 'z', split_axis=1, concat_axis=0, tiled=True)]
    ppermute x19 -> x27, waiting for transfers between devices: 78.7 us -> 105 us  [shifted(): return lax.ppermute(x, axis, [(i, (i + by) % count) for i in range(count)])]
    ppermute x1, waiting for transfers between devices: 15.9 us -> 0.01 us  [on_device(): g_col = lax.ppermute(g_col, line, in_plane)]
    all_to_all x4 -> x0, starting transfers between devices: 15.7 us -> none  [by_head(): return lax.all_to_all(x, 'z', split_axis=1, concat_axis=0, tiled=True)]
    pallas_call x2 -> x6, Pallas kernels: 22.6 us -> 35.4 us  [the longest x4 30.7 us: factor_part(): pl.pallas_call(kernel, out_shape=jax.ShapeDtypeStruct((8 * HEAD_DIM, 4 *...]
    pallas_call x1, Pallas kernels: 16.5 us -> 21.9 us  [attention(): pl.pallas_call(attention_kernel, out_shape=(jax.ShapeDtypeStruct((HEAD_DI...]
    unnamed x38 -> x54, local copies, waits for them, and re-layouts: 3.32 us -> 6.97 us
    all_to_all x4 -> x0, local copies, waits for them, and re-layouts: 3.54 us -> none  [by_head(): return lax.all_to_all(x, 'z', split_axis=1, concat_axis=0, tiled=True)]
  transfers between devices with their start and end apart: 29 -> 33, of which waited for: 16 -> 12; matrix products, arithmetic and copies ran while one was open for 4% -> 2% of each run, Pallas kernels for 7% -> 13%
where the time goes in v3:
time: 252 us; the launch traced here: 250 us
  waiting for transfers between devices  105 us (42%)
  Pallas kernels  63.4 us (25%)
  starting transfers between devices  53.4 us (21%)
  between operations  14.5 us (6%)
  local copies, waits for them, and re-layouts  10.5 us (4%)
    ppermute x27, waiting for transfers between devices, shifted(): return lax.ppermute(x, axis, [(i, (i + by) % count) for i in range(count)])  105 us
    ppermute x27, starting transfers between devices, shifted(): return lax.ppermute(x, axis, [(i, (i + by) % count) for i in range(count)])  42 us
    pallas_call x4, Pallas kernels, factor_part(): pl.pallas_call(kernel, out_shape=jax.ShapeDtypeStruct((8 * HEAD_DIM, 4 *...  30.7 us
    pallas_call x1, Pallas kernels, attention(): pl.pallas_call(attention_kernel, out_shape=(jax.ShapeDtypeStruct((HEAD_DI...  21.9 us
    unnamed x54, local copies, waits for them, and re-layouts  6.97 us
    ppermute x1, starting transfers between devices, on_device(): a_col = lax.ppermute(a_col, line, in_plane)  6.15 us
    pallas_call x2, Pallas kernels, stacked(): pl.pallas_call(stack_kernel, out_shape=jax.ShapeDtypeStruct((rows, *parts...  6.06 us
  transfers between devices with their start and end apart: 33, of which 12 were waited for; matrix products, arithmetic and copies ran while one was open for 2% of the time, Pallas kernels for 13%

profile of v3, /device:TPU:24, one launch (start us, length us, event | category | flops | bytes accessed | tf_op | source)
XLA Modules:
  0.0 249.5 jit_solution(17090898056939692563)
XLA Ops:
  16.2 3.2 %collective-permute-start.1 = (bf16[1024,128]{1,0:T(8,128)(2,1)}, bf16[1024,128]{1,0:T(8,128)(2,1)S(1)}, u32[]{:S(2)}, u32[]{:S(2)}) collective-permute-start(bf16[1024,128]{1,0:T(8,128)(2,1)} %get-tuple-element.37), channel_id=1, source_target_pairs={{0,6},{2,0},{4,2},{6,4},{1,7},{3,1},{5,3},{7,5},{8,14},{10,8},{12,... | collective-permute-start | bytes 786440 | tf_op jit(solution)/shard_map/ppermute | solution.py:161
  23.0 3.0 %collective-permute-start.3 = (bf16[1024,128]{1,0:T(8,128)(2,1)}, bf16[1024,128]{1,0:T(8,128)(2,1)S(1)}, u32[]{:S(2)}, u32[]{:S(2)}) collective-permute-start(bf16[1024,128]{1,0:T(8,128)(2,1)} %get-tuple-element.35.refs_0_), channel_id=1, source_target_pairs={{0,8},{8,0},{1,9},{9,1},{2,10},{10,2},{3,11},{11,3},{4,12},{12,4},... | collective-permute-start | bytes 786440 | tf_op jit(solution)/shard_map/ppermute | solution.py:161
  26.0 2.8 %collective-permute-start.4 = (bf16[1024,128]{1,0:T(8,128)(2,1)S(1)}, bf16[1024,128]{1,0:T(8,128)(2,1)S(1)}, u32[]{:S(2)}, u32[]{:S(2)}) collective-permute-start(bf16[1024,128]{1,0:T(8,128)(2,1)S(1)} %collective-permute-done.refs_1_), channel_id=1, source_target_pairs={{0,8},{8,0},{1,9},{9,1},{2,10},{10,2},{3,11},{11,3},{4,12},{12,4},... | collective-permute-start | bytes 786440 | tf_op jit(solution)/shard_map/ppermute | solution.py:161
  28.9 7.7 %collective-permute-done.1.refs_2_ = bf16[1024,128]{1,0:T(8,128)(2,1)S(1)} collective-permute-done((bf16[1024,128]{1,0:T(8,128)(2,1)}, bf16[1024,128]{1,0:T(8,128)(2,1)S(1)}, u32[]{:S(2)}, u32[]{:S(2)}) %collective-permute-start.1) | collective-permute-done | bytes 262176 | tf_op jit(solution)/shard_map/ppermute | solution.py:161
  36.5 3.0 %collective-permute-start.5 = (bf16[1024,128]{1,0:T(8,128)(2,1)S(1)}, bf16[1024,128]{1,0:T(8,128)(2,1)S(1)}, u32[]{:S(2)}, u32[]{:S(2)}) collective-permute-start(bf16[1024,128]{1,0:T(8,128)(2,1)S(1)} %collective-permute-done.1.refs_2_), channel_id=1, source_target_pairs={{0,8},{8,0},{1,9},{9,1},{2,10},{10,2},{3,11},{11,3},{4,12},{12,4},... | collective-permute-start | bytes 786440 | tf_op jit(solution)/shard_map/ppermute | solution.py:161
  40.7 4.7 %collective-permute-done.5.refs_6_ = bf16[1024,128]{1,0:T(8,128)(2,1)S(1)} collective-permute-done((bf16[1024,128]{1,0:T(8,128)(2,1)S(1)}, bf16[1024,128]{1,0:T(8,128)(2,1)S(1)}, u32[]{:S(2)}, u32[]{:S(2)}) %collective-permute-start.5) | collective-permute-done | bytes 262176 | tf_op jit(solution)/shard_map/ppermute | solution.py:161
  45.4 2.8 %collective-permute-done.6.refs_7_ = bf16[1024,128]{1,0:T(8,128)(2,1)S(1)} collective-permute-done((bf16[1024,128]{1,0:T(8,128)(2,1)S(1)}, bf16[1024,128]{1,0:T(8,128)(2,1)S(1)}, u32[]{:S(2)}, u32[]{:S(2)}) %collective-permute-start.6) | collective-permute-done | bytes 262176 | tf_op jit(solution)/shard_map/ppermute | solution.py:161
  48.9 21.9 %attention.1 = (bf16[128,2048]{1,0:T(8,128)(2,1)}, f32[128,2048]{1,0:T(8,128)}, bf16[128,2048]{1,0:T(8,128)(2,1)}) custom-call(s32[6]{0:T(128)} %starts.1, s32[2]{0:T(128)} %pad_add_fusion.1.where_ref, bf16[1024,128]{1,0:T(8,128)(2,1)} %get-tuple-element.35.refs_0_, bf16[1024,128]{1,0:T(8,128)(2,1)} %copy-done.15, bf16[1024,128]{1,0:T(8,128)(2,1)} %copy-done.16, ...), custom_call_target="tpu_custom_call" | custom-call | tf_op jit(solution)/shard_map/attention/pallas_call | solution.py:135
  72.6 3.8 %collective-permute-start.12 = (bf16[128,2048]{1,0:T(8,128)(2,1)}, bf16[128,2048]{1,0:T(8,128)(2,1)S(1)}, u32[]{:S(2)}, u32[]{:S(2)}) collective-permute-start(bf16[128,2048]{1,0:T(8,128)(2,1)} %get-tuple-element.46.refs_0_), channel_id=1, source_target_pairs={{0,6},{2,0},{4,2},{6,4},{1,7},{3,1},{5,3},{7,5},{8,14},{10,8},{12,... | collective-permute-start | bytes 1572872 | tf_op jit(solution)/shard_map/ppermute | solution.py:161
  76.4 5.4 %collective-permute-done.10 = bf16[128,2048]{1,0:T(8,128)(2,1)S(1)} collective-permute-done((bf16[128,2048]{1,0:T(8,128)(2,1)}, bf16[128,2048]{1,0:T(8,128)(2,1)S(1)}, u32[]{:S(2)}, u32[]{:S(2)}) %collective-permute-start.10) | collective-permute-done | bytes 524320 | tf_op jit(solution)/shard_map/ppermute | solution.py:161
  81.8 4.4 %collective-permute-done.12.refs_2_ = bf16[128,2048]{1,0:T(8,128)(2,1)S(1)} collective-permute-done((bf16[128,2048]{1,0:T(8,128)(2,1)}, bf16[128,2048]{1,0:T(8,128)(2,1)S(1)}, u32[]{:S(2)}, u32[]{:S(2)}) %collective-permute-start.12) | collective-permute-done | bytes 524320 | tf_op jit(solution)/shard_map/ppermute | solution.py:161
  87.1 2.9 %collective-permute-start.15 = (bf16[64,2048]{1,0:T(8,128)(2,1)S(1)}, bf16[64,2048]{1,0:T(8,128)(2,1)S(1)}, u32[]{:S(2)}, u32[]{:S(2)}) collective-permute-start(bf16[64,2048]{1,0:T(8,128)(2,1)S(1)} %slice.25), channel_id=1, source_target_pairs={{0,6},{2,0},{4,2},{6,4},{1,7},{3,1},{5,3},{7,5},{8,14},{10,8},{12,... | collective-permute-start | bytes 786440 | tf_op jit(solution)/shard_map/ppermute | solution.py:161
  92.8 3.9 %collective-permute-start.18 = (bf16[128,2048]{1,0:T(8,128)(2,1)S(1)}, bf16[128,2048]{1,0:T(8,128)(2,1)S(1)}, u32[]{:S(2)}, u32[]{:S(2)}) collective-permute-start(bf16[128,2048]{1,0:T(8,128)(2,1)S(1)} %add_convert_fusion.refs_0_), channel_id=1, source_target_pairs={{0,9},{1,0},{8,1},{9,8},{2,11},{3,2},{10,3},{11,10},{4,13},{5,4},{... | collective-permute-start | bytes 1572872 | tf_op jit(solution)/shard_map/ppermute | solution.py:161
  96.7 6.2 %collective-permute-start.16 = (bf16[128,2048]{1,0:T(8,128)(2,1)S(1)}, bf16[128,2048]{1,0:T(8,128)(2,1)S(1)}, u32[]{:S(2)}, u32[]{:S(2)}) collective-permute-start(bf16[128,2048]{1,0:T(8,128)(2,1)S(1)} %collective-permute-done.13), channel_id=1, source_target_pairs={{0,0},{34,32},{68,64},{102,96},{8,16},{42,48},{76,80},{110,112},{1... | collective-permute-start | bytes 1572872 | tf_op jit(solution)/shard_map/ppermute | solution.py:356
  103.0 17.2 %collective-permute-done.14.refs_3_ = bf16[64,2048]{1,0:T(8,128)(2,1)S(1)} collective-permute-done((bf16[64,2048]{1,0:T(8,128)(2,1)S(1)}, bf16[64,2048]{1,0:T(8,128)(2,1)S(1)}, u32[]{:S(2)}, u32[]{:S(2)}) %collective-permute-start.14) | collective-permute-done | bytes 262176 | tf_op jit(solution)/shard_map/ppermute | solution.py:161
  121.9 3.0 %stack.23.refs_0_ = bf16[512,2048]{1,0:T(8,128)(2,1)} custom-call(bf16[128,2048]{1,0:T(8,128)(2,1)} %get-tuple-element.46.refs_0_, bf16[128,2048]{1,0:T(8,128)(2,1)} %copy-done.7, bf16[128,2048]{1,0:T(8,128)(2,1)} %copy-done.6, bf16[64,2048]{1,0:T(8,128)(2,1)} %copy-done.24, bf16[64,2048]{1,0:T(8,128)(2,1)} %copy-done.20), custom_call_target="tpu_custom_call" | custom-call | tf_op jit(solution)/shard_map/stack/pallas_call | solution.py:221
  129.0 14.0 %collective-permute-done.25.refs_4_ = bf16[64,2048]{1,0:T(8,128)(2,1)S(1)} collective-permute-done((bf16[64,2048]{1,0:T(8,128)(2,1)S(1)}, bf16[64,2048]{1,0:T(8,128)(2,1)S(1)}, u32[]{:S(2)}, u32[]{:S(2)}) %collective-permute-start.25) | collective-permute-done | bytes 262176 | tf_op jit(solution)/shard_map/ppermute | solution.py:161
  144.4 3.1 %stack.24.refs_0_ = bf16[512,2048]{1,0:T(8,128)(2,1)} custom-call(bf16[128,2048]{1,0:T(8,128)(2,1)} %copy-done.5, bf16[128,2048]{1,0:T(8,128)(2,1)} %copy-done.9, bf16[128,2048]{1,0:T(8,128)(2,1)} %copy-done.8, bf16[64,2048]{1,0:T(8,128)(2,1)} %copy-done.26, bf16[64,2048]{1,0:T(8,128)(2,1)} %copy-done.25), custom_call_target="tpu_custom_call" | custom-call | tf_op jit(solution)/shard_map/stack/pallas_call | solution.py:221
  152.3 43.1 %collective-permute-done.22.refs_1_ = bf16[512,2048]{1,0:T(8,128)(2,1)S(1)} collective-permute-done((bf16[512,2048]{1,0:T(8,128)(2,1)S(1)}, bf16[512,2048]{1,0:T(8,128)(2,1)S(1)}, u32[]{:S(2)}, u32[]{:S(2)}) %collective-permute-start.22) | collective-permute-done | bytes 2097184 | tf_op jit(solution)/shard_map/ppermute | solution.py:161
  206.7 7.7 %input_near.1.refs_4_ = f32[1024,512]{1,0:T(8,128)} custom-call(s32[2]{0:T(128)} %pad_add_fusion.place, bf16[512,2048]{1,0:T(8,128)(2,1)} %copy-done.4, bf16[512,2048]{1,0:T(8,128)(2,1)} %copy-done.3, bf16[1024,2048]{1,0:T(8,128)(2,1)} %all-gather.3.cloned.1.call-done.refs_2_.refs_3_), custom_call_target="tpu_custom_call" | custom-call | tf_op jit(solution)/shard_map/input_near/pallas_call | solution.py:308
  214.4 9.5 %grad_near.1.refs_3_ = f32[1024,512]{1,0:T(8,128)} custom-call(s32[2]{0:T(128)} %pad_add_fusion.place, bf16[512,2048]{1,0:T(8,128)(2,1)} %stack.24.refs_0_, bf16[512,2048]{1,0:T(8,128)(2,1)} %copy-done.2, bf16[512,2048]{1,0:T(8,128)(2,1)} %copy-done.1, bf16[1024,2048]{1,0:T(8,128)(2,1)} %all-gather.5.cloned.1.call-done.refs_3_.refs_2_), custom_call_target="tpu_custom_call" | custom-call | tf_op jit(solution)/shard_map/grad_near/pallas_call | solution.py:308
  223.9 3.2 %collective-permute-done.29.refs_0_ = bf16[256,2048]{1,0:T(8,128)(2,1)} collective-permute-done((bf16[256,2048]{1,0:T(8,128)(2,1)}, bf16[256,2048]{1,0:T(8,128)(2,1)}, u32[]{:S(2)}, u32[]{:S(2)}) %collective-permute-start.29) | collective-permute-done | bytes 1048608 | tf_op jit(solution)/shard_map/ppermute | solution.py:161
  227.2 5.8 %grad_far.1 = f32[1024,512]{1,0:T(8,128)} custom-call(s32[2]{0:T(128)} %pad_add_fusion.place, bf16[256,2048]{1,0:T(8,128)(2,1)} %collective-permute-done.29.refs_0_, bf16[256,2048]{1,0:T(8,128)(2,1)} %collective-permute-done.30.refs_1_, bf16[1024,2048]{1,0:T(8,128)(2,1)} %all-gather.5.cloned.1.call-done.refs_3_.refs_2_, ...), custom_call_target="tpu_custom_call", output_to_operand_aliasing={{}: (4, {})} | custom-call | tf_op jit(solution)/shard_map/grad_far/pallas_call | solution.py:308
  235.0 7.7 %input_far.1 = f32[1024,512]{1,0:T(8,128)} custom-call(s32[2]{0:T(128)} %pad_add_fusion.place, bf16[512,2048]{1,0:T(8,128)(2,1)} %stack.23.refs_0_, bf16[256,2048]{1,0:T(8,128)(2,1)} %copy-done.11, bf16[256,2048]{1,0:T(8,128)(2,1)} %copy-done.10, bf16[1024,2048]{1,0:T(8,128)(2,1)} %all-gather.3.cloned.1.call-done.refs_2_.refs_3_, ...), custom_call_target="tpu_custom_call", output_to_operand_aliasing={{}: (5, {})} | custom-call | tf_op jit(solution)/shard_map/input_far/pallas_call | solution.py:308
  (118 shorter events, 45.0 us)
Async XLA Ops:
  7.2 199.5 %all-gather.3.cloned.1.call-start = ((), (), s32[]{:S(2)}) async-start(), calls=%async_computation | async-start | bytes 4718592 | tf_op jit(solution)/shard_map/all_gather | solution.py:365
  16.2 20.3 %collective-permute-start.1 = (bf16[1024,128]{1,0:T(8,128)(2,1)}, bf16[1024,128]{1,0:T(8,128)(2,1)S(1)}, u32[]{:S(2)}, u32[]{:S(2)}) collective-permute-start(bf16[1024,128]{1,0:T(8,128)(2,1)} %get-tuple-element.37), channel_id=1, source_target_pairs={{0,6},{2,0},{4,2},{6,4},{1,7},{3,1},{5,3},{7,5},{8,14},{10,8},{12,... | collective-permute-start | bytes 786440 | tf_op jit(solution)/shard_map/ppermute | solution.py:161
  19.4 20.1 %collective-permute-start.2 = (bf16[1024,128]{1,0:T(8,128)(2,1)}, bf16[1024,128]{1,0:T(8,128)(2,1)S(1)}, u32[]{:S(2)}, u32[]{:S(2)}) collective-permute-start(bf16[1024,128]{1,0:T(8,128)(2,1)} %get-tuple-element.38), channel_id=1, source_target_pairs={{0,4},{2,6},{4,0},{6,2},{1,5},{3,7},{5,1},{7,3},{8,12},{10,14},{12... | collective-permute-start | bytes 786440 | tf_op jit(solution)/shard_map/ppermute | solution.py:161
  20.6 20.1 %collective-permute-start.9 = (bf16[1024,128]{1,0:T(8,128)(2,1)}, bf16[1024,128]{1,0:T(8,128)(2,1)S(1)}, u32[]{:S(2)}, u32[]{:S(2)}) collective-permute-start(bf16[1024,128]{1,0:T(8,128)(2,1)} %get-tuple-element.42), channel_id=1, source_target_pairs={{0,4},{2,6},{4,0},{6,2},{1,5},{3,7},{5,1},{7,3},{8,12},{10,14},{12... | collective-permute-start | bytes 786440 | tf_op jit(solution)/shard_map/ppermute | solution.py:161
  23.0 17.7 %collective-permute-start.3 = (bf16[1024,128]{1,0:T(8,128)(2,1)}, bf16[1024,128]{1,0:T(8,128)(2,1)S(1)}, u32[]{:S(2)}, u32[]{:S(2)}) collective-permute-start(bf16[1024,128]{1,0:T(8,128)(2,1)} %get-tuple-element.35.refs_0_), channel_id=1, source_target_pairs={{0,8},{8,0},{1,9},{9,1},{2,10},{10,2},{3,11},{11,3},{4,12},{12,4},... | collective-permute-start | bytes 786440 | tf_op jit(solution)/shard_map/ppermute | solution.py:161
  26.0 14.7 %collective-permute-start.4 = (bf16[1024,128]{1,0:T(8,128)(2,1)S(1)}, bf16[1024,128]{1,0:T(8,128)(2,1)S(1)}, u32[]{:S(2)}, u32[]{:S(2)}) collective-permute-start(bf16[1024,128]{1,0:T(8,128)(2,1)S(1)} %collective-permute-done.refs_1_), channel_id=1, source_target_pairs={{0,8},{8,0},{1,9},{9,1},{2,10},{10,2},{3,11},{11,3},{4,12},{12,4},... | collective-permute-start | bytes 786440 | tf_op jit(solution)/shard_map/ppermute | solution.py:161
  87.1 15.8 %collective-permute-start.15 = (bf16[64,2048]{1,0:T(8,128)(2,1)S(1)}, bf16[64,2048]{1,0:T(8,128)(2,1)S(1)}, u32[]{:S(2)}, u32[]{:S(2)}) collective-permute-start(bf16[64,2048]{1,0:T(8,128)(2,1)S(1)} %slice.25), channel_id=1, source_target_pairs={{0,6},{2,0},{4,2},{6,4},{1,7},{3,1},{5,3},{7,5},{8,14},{10,8},{12,... | collective-permute-start | bytes 786440 | tf_op jit(solution)/shard_map/ppermute | solution.py:161
  91.3 28.9 %collective-permute-start.19 = (bf16[128,2048]{1,0:T(8,128)(2,1)S(1)}, bf16[128,2048]{1,0:T(8,128)(2,1)}, u32[]{:S(2)}, u32[]{:S(2)}) collective-permute-start(bf16[128,2048]{1,0:T(8,128)(2,1)S(1)} %add_convert_fusion.refs_0_), channel_id=1, source_target_pairs={{0,0},{2,34},{4,68},{6,102},{8,8},{10,42},{12,76},{14,110},{16,16}... | collective-permute-start | bytes 1572872 | tf_op jit(solution)/shard_map/ppermute | solution.py:354
  92.8 27.4 %collective-permute-start.18 = (bf16[128,2048]{1,0:T(8,128)(2,1)S(1)}, bf16[128,2048]{1,0:T(8,128)(2,1)S(1)}, u32[]{:S(2)}, u32[]{:S(2)}) collective-permute-start(bf16[128,2048]{1,0:T(8,128)(2,1)S(1)} %add_convert_fusion.refs_0_), channel_id=1, source_target_pairs={{0,9},{1,0},{8,1},{9,8},{2,11},{3,2},{10,3},{11,10},{4,13},{5,4},{... | collective-permute-start | bytes 1572872 | tf_op jit(solution)/shard_map/ppermute | solution.py:161
  96.7 23.5 %collective-permute-start.17 = (bf16[128,2048]{1,0:T(8,128)(2,1)S(1)}, bf16[128,2048]{1,0:T(8,128)(2,1)S(1)}, u32[]{:S(2)}, u32[]{:S(2)}) collective-permute-start(bf16[128,2048]{1,0:T(8,128)(2,1)S(1)} %add_convert_fusion.refs_0_), channel_id=1, source_target_pairs={{0,1},{1,8},{8,9},{9,0},{2,3},{3,10},{10,11},{11,2},{4,5},{5,12},{... | collective-permute-start | bytes 1572872 | tf_op jit(solution)/shard_map/ppermute | solution.py:161
  96.7 24.2 %collective-permute-start.16 = (bf16[128,2048]{1,0:T(8,128)(2,1)S(1)}, bf16[128,2048]{1,0:T(8,128)(2,1)S(1)}, u32[]{:S(2)}, u32[]{:S(2)}) collective-permute-start(bf16[128,2048]{1,0:T(8,128)(2,1)S(1)} %collective-permute-done.13), channel_id=1, source_target_pairs={{0,0},{34,32},{68,64},{102,96},{8,16},{42,48},{76,80},{110,112},{1... | collective-permute-start | bytes 1572872 | tf_op jit(solution)/shard_map/ppermute | solution.py:356
  102.9 17.3 %collective-permute-start.14 = (bf16[64,2048]{1,0:T(8,128)(2,1)S(1)}, bf16[64,2048]{1,0:T(8,128)(2,1)S(1)}, u32[]{:S(2)}, u32[]{:S(2)}) collective-permute-start(bf16[64,2048]{1,0:T(8,128)(2,1)S(1)} %slice.24), channel_id=1, source_target_pairs={{0,2},{2,4},{4,6},{6,0},{1,3},{3,5},{5,7},{7,1},{8,10},{10,12},{12... | collective-permute-start | bytes 786440 | tf_op jit(solution)/shard_map/ppermute | solution.py:161
  121.8 92.5 %all-gather.5.cloned.1.call-start = ((), (), s32[]{:S(2)}) async-start(), calls=%async_computation.1 | async-start | bytes 4718592 | tf_op jit(solution)/shard_map/all_gather | solution.py:369
  124.9 22.7 %collective-permute-start.28 = (bf16[128,2048]{1,0:T(8,128)(2,1)}, bf16[128,2048]{1,0:T(8,128)(2,1)}, u32[]{:S(2)}, u32[]{:S(2)}) collective-permute-start(bf16[128,2048]{1,0:T(8,128)(2,1)} %collective-permute-done.19), channel_id=1, source_target_pairs={{0,0},{34,32},{68,64},{102,96},{8,16},{42,48},{76,80},{110,112},{1... | collective-permute-start | bytes 1572872 | tf_op jit(solution)/shard_map/ppermute | solution.py:364
  126.9 16.1 %collective-permute-start.25 = (bf16[64,2048]{1,0:T(8,128)(2,1)S(1)}, bf16[64,2048]{1,0:T(8,128)(2,1)S(1)}, u32[]{:S(2)}, u32[]{:S(2)}) collective-permute-start(bf16[64,2048]{1,0:T(8,128)(2,1)S(1)} %slice.29), channel_id=1, source_target_pairs={{0,9},{1,0},{8,1},{9,8},{2,11},{3,2},{10,3},{11,10},{4,13},{5,4},{... | collective-permute-start | bytes 786440 | tf_op jit(solution)/shard_map/ppermute | solution.py:161
  127.0 16.0 %collective-permute-start.24 = (bf16[64,2048]{1,0:T(8,128)(2,1)S(1)}, bf16[64,2048]{1,0:T(8,128)(2,1)S(1)}, u32[]{:S(2)}, u32[]{:S(2)}) collective-permute-start(bf16[64,2048]{1,0:T(8,128)(2,1)S(1)} %slice.28), channel_id=1, source_target_pairs={{0,1},{1,8},{8,9},{9,0},{2,3},{3,10},{10,11},{11,2},{4,5},{5,12},{... | collective-permute-start | bytes 786440 | tf_op jit(solution)/shard_map/ppermute | solution.py:161
  147.6 47.8 %collective-permute-start.22 = (bf16[512,2048]{1,0:T(8,128)(2,1)S(1)}, bf16[512,2048]{1,0:T(8,128)(2,1)S(1)}, u32[]{:S(2)}, u32[]{:S(2)}) collective-permute-start(bf16[512,2048]{1,0:T(8,128)(2,1)S(1)} %copy-done), channel_id=1, source_target_pairs={{0,9},{1,0},{8,1},{9,8},{2,11},{3,2},{10,3},{11,10},{4,13},{5,4},{... | collective-permute-start | bytes 6291464 | tf_op jit(solution)/shard_map/ppermute | solution.py:161
  150.3 47.5 %collective-permute-start.27 = (bf16[512,2048]{1,0:T(8,128)(2,1)}, bf16[512,2048]{1,0:T(8,128)(2,1)S(1)}, u32[]{:S(2)}, u32[]{:S(2)}) collective-permute-start(bf16[512,2048]{1,0:T(8,128)(2,1)} %stack.24.refs_0_), channel_id=1, source_target_pairs={{0,6},{2,0},{4,2},{6,4},{1,7},{3,1},{5,3},{7,5},{8,14},{10,8},{12,... | collective-permute-start | bytes 6291464 | tf_op jit(solution)/shard_map/ppermute | solution.py:161
  150.3 50.2 %collective-permute-start.26 = (bf16[512,2048]{1,0:T(8,128)(2,1)}, bf16[512,2048]{1,0:T(8,128)(2,1)S(1)}, u32[]{:S(2)}, u32[]{:S(2)}) collective-permute-start(bf16[512,2048]{1,0:T(8,128)(2,1)} %stack.24.refs_0_), channel_id=1, source_target_pairs={{0,2},{2,4},{4,6},{6,0},{1,3},{3,5},{5,7},{7,1},{8,10},{10,12},{12... | collective-permute-start | bytes 6291464 | tf_op jit(solution)/shard_map/ppermute | solution.py:161
  152.3 52.3 %collective-permute-start.20 = (bf16[512,2048]{1,0:T(8,128)(2,1)S(1)}, bf16[512,2048]{1,0:T(8,128)(2,1)S(1)}, u32[]{:S(2)}, u32[]{:S(2)}) collective-permute-start(bf16[512,2048]{1,0:T(8,128)(2,1)S(1)} %copy-done), channel_id=1, source_target_pairs={{0,1},{1,8},{8,9},{9,0},{2,3},{3,10},{10,11},{11,2},{4,5},{5,12},{... | collective-permute-start | bytes 6291464 | tf_op jit(solution)/shard_map/ppermute | solution.py:161
  199.0 25.0 %collective-permute-start.30 = (bf16[256,2048]{1,0:T(8,128)(2,1)}, bf16[256,2048]{1,0:T(8,128)(2,1)}, u32[]{:S(2)}, u32[]{:S(2)}) collective-permute-start(bf16[256,2048]{1,0:T(8,128)(2,1)} %slice.35), channel_id=1, source_target_pairs={{0,6},{2,0},{4,2},{6,4},{1,7},{3,1},{5,3},{7,5},{8,14},{10,8},{12,... | collective-permute-start | bytes 3145736 | tf_op jit(solution)/shard_map/ppermute | solution.py:161
  201.6 25.5 %collective-permute-start.29 = (bf16[256,2048]{1,0:T(8,128)(2,1)}, bf16[256,2048]{1,0:T(8,128)(2,1)}, u32[]{:S(2)}, u32[]{:S(2)}) collective-permute-start(bf16[256,2048]{1,0:T(8,128)(2,1)} %slice.34), channel_id=1, source_target_pairs={{0,2},{2,4},{4,6},{6,0},{1,3},{3,5},{5,7},{7,1},{8,10},{10,12},{12... | collective-permute-start | bytes 3145736 | tf_op jit(solution)/shard_map/ppermute | solution.py:161
  202.1 30.8 %collective-permute-start.23 = (bf16[256,2048]{1,0:T(8,128)(2,1)}, bf16[256,2048]{1,0:T(8,128)(2,1)S(1)}, u32[]{:S(2)}, u32[]{:S(2)}) collective-permute-start(bf16[256,2048]{1,0:T(8,128)(2,1)} %slice.33), channel_id=1, source_target_pairs={{0,9},{1,0},{8,1},{9,8},{2,11},{3,2},{10,3},{11,10},{4,13},{5,4},{... | collective-permute-start | bytes 3145736 | tf_op jit(solution)/shard_map/ppermute | solution.py:161
  206.0 27.0 %collective-permute-start.21 = (bf16[256,2048]{1,0:T(8,128)(2,1)S(1)}, bf16[256,2048]{1,0:T(8,128)(2,1)S(1)}, u32[]{:S(2)}, u32[]{:S(2)}) collective-permute-start(bf16[256,2048]{1,0:T(8,128)(2,1)S(1)} %slice.32), channel_id=1, source_target_pairs={{0,1},{1,8},{8,9},{9,0},{2,3},{3,10},{10,11},{11,2},{4,5},{5,12},{... | collective-permute-start | bytes 3145736 | tf_op jit(solution)/shard_map/ppermute | solution.py:161
  (36 other events, 393.0 us)
Sparse Core Ops, SparseCore 0:
  122.0 27.9 all-gather.2
  151.7 32.0 all-gather.4
